TPU v7x, 128 devices: a whole 4x4x4 slice. The times are simulated.
128 devices in a mesh: gx: 8 (over y, core), gy: 16 (over z, x).
Axes of the slice: x: 4, y: 4, z: 4, core: 2. Of those that a mesh axis runs over, the one named last changes fastest.
Arguments:
- features: bfloat16 [1024, 110592], P('gx', 'gy'), may hold values from -6 to 6
- first_weight: bfloat16 [110592, 768], P(('gy', 'gx')), may hold values from -0.01953125 to 0.01953125
- second_weight: bfloat16 [768, 512], replicated, may hold values from -0.21875 to 0.21875
- centres: bfloat16 [622592, 512], P(('gx', 'gy')), may hold values from -6 to 6
- active: int32 [622592], P(('gx', 'gy')), may hold values from 0 to 16127, as said below
- labels: int32 [1024], replicated, may hold values from 0 to 2064383, as said below
Outputs:
- loss: float32 [], replicated
- grad_first: bfloat16 [110592, 768], P(('gy', 'gx'))
- grad_second: bfloat16 [768, 512], replicated
- grad_centres: bfloat16 [622592, 512], P(('gx', 'gy'))
Inputs may be any that keep to these rules, and one draw needn't show every extreme that they name: Each shard's 4864 entries are distinct and increasing; entry c names class (c // 4864) * 16128 + active[c]. `labels`: every image's class is among the sampled classes, so exactly one centre matches it.
All inputs are finite; a program needn't handle non-finite values.
Results may differ from a plain program's by a relative error of at most 0.0075.
Values may be sent and summed in bfloat16 or wider, within the bound.
A program may use at most 128 MiB of HBM per device.

v0:
```python
import jax
import jax.numpy as jnp
from jax import lax
from jax.sharding import PartitionSpec as P

CLS_DEV = 16128


LOGIT_SCALE = 64.0
COS_MARGIN = 0.4
NORM_EPSILON = 1e-06


def shards(features, first_weight, second_weight, centres, active, labels):
    gy_count = lax.axis_size("gy")
    device = lax.axis_index("gx") * gy_count + lax.axis_index("gy")
    image_count = labels.shape[0]
    spread = lax.all_to_all(features, "gx", split_axis=1, concat_axis=0, tiled=True)
    block_rows = spread
    hidden = lax.psum_scatter(
        jnp.dot(block_rows, first_weight, preferred_element_type=jnp.float32),
        ("gx", "gy"),
        scatter_dimension=0,
        tiled=True,
    )
    activation, gelu_back = jax.vjp(jax.nn.gelu, hidden)
    act_half = activation.astype(jnp.bfloat16)
    embedding = jnp.dot(act_half, second_weight, preferred_element_type=jnp.float32)
    inv_embed = lax.rsqrt(jnp.sum(embedding * embedding, axis=1, keepdims=True) + NORM_EPSILON)
    unit = embedding * inv_embed
    unit_half = unit.astype(jnp.bfloat16)
    unit_all = lax.all_gather(unit_half, ("gx", "gy"), axis=0, tiled=True)
    cen = centres.astype(jnp.float32)
    inv_cen = lax.rsqrt(jnp.sum(cen * cen, axis=1, keepdims=True) + NORM_EPSILON)
    normed = cen * inv_cen
    normed_half = normed.astype(jnp.bfloat16)
    cosine = jnp.dot(unit_all, normed_half.T, preferred_element_type=jnp.float32)
    classes = device * CLS_DEV + active
    matches = labels[:, None] == classes[None, :]
    positive = matches.astype(jnp.float32)
    logits = LOGIT_SCALE * (cosine - COS_MARGIN * positive)
    exp_terms = jnp.exp(logits - LOGIT_SCALE)
    row_total = jnp.sum(exp_terms, axis=1)
    row_target = jnp.sum(positive * logits, axis=1)
    weighted = jnp.dot(
        exp_terms.astype(jnp.bfloat16), normed_half, preferred_element_type=jnp.float32
    )
    found = jnp.any(matches, axis=1)
    where_found = jnp.argmax(matches.astype(jnp.int32), axis=1)
    picked = normed_half[where_found].astype(jnp.float32) * found[:, None].astype(jnp.float32)
    totals, target = lax.psum((row_total, row_target), ("gx", "gy"))
    factor = LOGIT_SCALE / image_count
    term = factor * (weighted / totals[:, None] - picked)
    grad_unit = lax.psum_scatter(term, ("gx", "gy"), scatter_dimension=0, tiled=True)
    coeff = (factor * (exp_terms / totals[:, None] - positive)).astype(jnp.bfloat16)
    grad_normed = jnp.dot(coeff.T, unit_all, preferred_element_type=jnp.float32)
    grad_cen = inv_cen * (
        grad_normed - normed * jnp.sum(grad_normed * normed, axis=1, keepdims=True)
    )
    loss = jnp.mean(LOGIT_SCALE + jnp.log(totals) - target)
    grad_embed = inv_embed * (grad_unit - unit * jnp.sum(grad_unit * unit, axis=1, keepdims=True))
    grad_embed_half = grad_embed.astype(jnp.bfloat16)
    second_term = jnp.dot(act_half.T, grad_embed_half, preferred_element_type=jnp.float32)
    grad_second = lax.psum(second_term, ("gx", "gy"))
    grad_act = jnp.dot(grad_embed_half, second_weight.T, preferred_element_type=jnp.float32)
    (grad_hidden,) = gelu_back(grad_act)
    grad_hidden_half = grad_hidden.astype(jnp.bfloat16)
    block_rows = spread
    grad_first = jnp.dot(
        block_rows.T,
        lax.all_gather(grad_hidden_half, ("gx", "gy"), axis=0, tiled=True),
        preferred_element_type=jnp.float32,
    )
    return (
        loss,
        grad_first.astype(jnp.bfloat16),
        grad_second.astype(jnp.bfloat16),
        grad_cen.astype(jnp.bfloat16),
    )


def solution(mesh):
    placed = (
        P("gx", "gy"),
        P(("gy", "gx"), None),
        P(),
        P(("gx", "gy"), None),
        P(("gx", "gy")),
        P(),
    )
    return jax.shard_map(
        shards,
        mesh=mesh,
        in_specs=placed,
        out_specs=(P(), P(("gy", "gx"), None), P(), P(("gx", "gy"), None)),
        check_vma=False,
    )
```

profile of v0, /device:TPU:1, one launch (start us, length us, event | category | flops | bytes accessed | tf_op | source)
XLA Modules:
  0.0 1172.7 jit_solution(1254652785971948918)
XLA Ops:
  7.2 0.0 copy-start
  7.2 0.0 reduce-scatter.3.cloned.1.call-start
  7.2 2.8 copy.13
  10.1 28.5 %all_to_all.19 = bf16[128,8,864]{0,2,1:T(8,128)(2,1)S(1)} all-to-all(bf16[128,8,864]{0,2,1:T(8,128)(2,1)S(1)} %bitcast.32), channel_id=1, replica_groups=mesh['gx'=8,'gy'=16] {'gx'}, dimensions={1} | all-to-all | bytes 3538944 | tf_op jit(solution)/shard_map/all_to_all | solution.py:18
  38.6 1.2 copy-done.4
  39.8 0.0 copy-done
  39.8 3.5 fusion.24
  43.3 0.0 reduce-scatter.3.cloned.1.call-update
  43.3 0.0 all-gather.3.cloned.1.call-start
  43.4 7.5 copy.15
  50.9 3.6 fusion.16
  54.5 0.3 copy-done.2
  54.9 3.0 fusion.11
  57.9 7.7 copy.16
  65.5 0.0 copy-done.6
  65.5 0.0 copy-done.7
  65.6 2.6 compare_reduce_fusion
  68.2 184.2 %reduce-scatter.3.cloned.1.call-done = f32[8,768]{1,0:T(8,128)} async-done(((f32[1024,768]{1,0:T(8,128)}), f32[8,768]{1,0:T(8,128)}) %reduce-scatter.3.cloned.1.call-update) | async-done | bytes 24592 | tf_op jit(solution)/shard_map/reduce_scatter | solution.py:20
  252.4 0.0 copy-done.3
  252.4 1.1 multiply_reduce_fusion.1
  253.5 0.7 multiply_convert_fusion.2
  254.2 0.0 all-gather.3.cloned.1.call-update
  254.2 0.2 reduce-scatter.5.cloned.1.call-start
  254.5 8.3 fusion.3
  262.8 7.0 gather_fusion
  269.8 49.6 %all-gather.3.cloned.1.call-done = bf16[1024,512]{1,0:T(8,128)(2,1)} async-done(((bf16[8,512]{1,0:T(8,128)(2,1)}), bf16[1024,512]{1,0:T(8,128)(2,1)}) %all-gather.3.cloned.1.call-update) | async-done | bytes 1048592 | tf_op jit(solution)/shard_map/all_gather | solution.py:32
  319.5 14.8 %fusion.8 = (f32[1024]{0:T(1024)S(1)}, f32[1024]{0:T(1024)S(1)}, f32[1024,4864]{1,0:T(8,128)}) fusion(s32[4864]{0:T(1024)S(1)} %broadcast_add_fusion, s32[1024]{0:T(1024)S(1)} %copy-done.7, bf16[1024,512]{1,0:T(8,128)(2,1)} %all-gather.3.cloned.1.call-done, bf16[4864,512]{0,1:T(8,128)(2,1)} %fusion.11), kind=kOutput, calls=%fused_computation.15 | convolution fusion | flops 5140117504 | bytes 25984000 | tf_op jit(solution)/shard_map/dot_general | solution.py:37
  334.3 62.3 %psum.21 = f32[1024]{0:T(1024)S(1)} all-reduce(f32[1024]{0:T(1024)S(1)} %get-tuple-element.14), channel_id=1, replica_groups=mesh['gx'=8,'gy'=16] {'gx','gy'}, use_global_device_ids=true, to_apply=%region_4.0 | all-reduce | flops 1024 | bytes 8192 | tf_op jit(solution)/shard_map/psum | solution.py:51
  396.6 12.0 %subtract_multiply_fusion = f32[1024,512]{1,0:T(8,128)} fusion(bf16[1024,512]{1,0:T(8,128)(2,1)S(1)} %gather_fusion, bf16[4864,512]{0,1:T(8,128)(2,1)} %fusion.11, f32[1024,4864]{1,0:T(8,128)} %get-tuple-element.20, f32[1024]{0:T(1024)S(1)} %convert_element_type.60, f32[1024]{0:T(1024)S(1)} %psum.21), kind=kOutput, calls=%fused_computation.29 | convolution fusion | flops 5112856576 | bytes 28057600 | tf_op jit(solution)/shard_map/dot_general | solution.py:45
  408.6 0.0 reduce-scatter.5.cloned.1.call-update
  408.6 0.0 all-gather.5.cloned.1.call-start
  408.7 613.9 %reduce-scatter.5.cloned.1.call-done = f32[8,512]{1,0:T(8,128)} async-done(((f32[1024,512]{1,0:T(8,128)}), f32[8,512]{1,0:T(8,128)}) %reduce-scatter.5.cloned.1.call-update) | async-done | bytes 16400 | tf_op jit(solution)/shard_map/reduce_scatter | solution.py:54
  1022.5 0.9 multiply_reduce_fusion
  1023.4 0.8 multiply_convert_fusion.1
  1024.2 0.0 copy-done.5
  1024.2 0.9 fusion.42
  1025.2 0.0 all-gather.5.cloned.1.call-update
  1025.2 0.0 slice-start.1
  1025.2 16.6 %fusion.12 = (f32[4864]{0:T(1024)S(1)}, f32[4864,512]{0,1:T(8,128)}) fusion(bf16[4864,512]{0,1:T(8,128)(2,1)} %copy.15, f32[4864]{0:T(1024)S(1)} %add_rsqrt_fusion, bf16[1024,512]{1,0:T(8,128)(2,1)} %all-gather.3.cloned.1.call-done, f32[1024,4864]{1,0:T(8,128)} %get-tuple-element.20, f32[1024]{0:T(1024)S(1)} %psum.21, s32[4864]{0:T(1024)S(1)} %broadcast_add_fusion, ...), kind=kOutput, calls=%fused_computation.21 | convolution fusion | flops 5145095168 | bytes 35980288 | tf_op jit(solution)/shard_map/dot_general | solution.py:56
  1041.8 0.0 slice-done
  1041.8 0.0 slice-done.1
  1041.8 7.9 fusion.15
  1049.7 7.6 copy.17
  1057.2 0.4 fusion.47
  1057.7 101.4 %all-reduce.2 = (f32[1024]{0:T(1024)S(1)}, bf16[768,512]{1,0:T(8,128)(2,1)}) all-reduce(f32[1024]{0:T(1024)S(1)} %get-tuple-element.15, f32[768,512]{1,0:T(8,128)S(1)} %fusion.47), channel_id=1, replica_groups=mesh['gx'=8,'gy'=16] {'gx','gy'}, use_global_device_ids=true, to_apply=%region_6.0 | all-reduce | flops 394240 | bytes 2367488 | tf_op jit(solution)/shard_map/psum | solution.py:51
  1159.1 0.6 subtract_reduce_fusion
  1160.4 0.0 all-gather.5.cloned.1.call-done
  1160.5 4.5 fusion.31
  (15 shorter events, 0.0 us)
Async XLA Ops:
  7.2 32.6 %copy-start = (bf16[864,768]{1,0:T(8,128)(2,1)S(1)}, bf16[864,768]{1,0:T(8,128)(2,1)}, u32[]{:S(2)}) copy-start(bf16[864,768]{1,0:T(8,128)(2,1)} %param.7) | copy-start | bytes 3981316
  7.2 245.3 %reduce-scatter.3.cloned.1.call-start = ((), (), s32[]{:S(2)}) async-start(), calls=%async_computation.3 | async-start | bytes 3170304 | tf_op jit(solution)/shard_map/reduce_scatter | solution.py:20
  38.6 1.2 copy-start.4
  43.3 276.2 %all-gather.3.cloned.1.call-start = ((), (), s32[]{:S(2)}) async-start(), calls=%async_computation.4 | async-start | bytes 1056768 | tf_op jit(solution)/shard_map/all_gather | solution.py:32
  50.9 3.9 copy-start.2
  57.9 7.7 copy-start.6
  57.9 7.7 copy-start.7
  57.9 194.6 %copy-start.3 = (bf16[768,512]{1,0:T(8,128)(2,1)S(1)}, bf16[768,512]{1,0:T(8,128)(2,1)}, u32[]{:S(2)}) copy-start(bf16[768,512]{1,0:T(8,128)(2,1)} %param.8) | copy-start | bytes 2359300
  254.2 768.3 %reduce-scatter.5.cloned.1.call-start = ((), (), s32[]{:S(2)}) async-start(), calls=%async_computation.5 | async-start | bytes 2113536 | tf_op jit(solution)/shard_map/reduce_scatter | solution.py:54
  396.6 627.6 %copy-start.5 = (f32[8,768]{1,0:T(8,128)S(1)}, f32[8,768]{1,0:T(8,128)}, u32[]{:S(2)}) copy-start(f32[8,768]{1,0:T(8,128)} %reduce-scatter.3.cloned.1.call-done) | copy-start | bytes 73732
  408.6 633.2 %slice-start = ((s8[4980736]{0:T(1024)(128)(4,1)}), s8[786432]{0:T(1024)(128)(4,1)S(1)}, s32[]{:S(2)}) async-start(s8[4980736]{0:T(1024)(128)(4,1)} %bitcast.30), calls=%async_computation.7 | async-start | bytes 1572864
  408.6 751.8 %all-gather.5.cloned.1.call-start = ((), (), s32[]{:S(2)}) async-start(), calls=%async_computation.6 | async-start | bytes 1585152 | tf_op jit(solution)/shard_map/all_gather | solution.py:71
  1025.2 16.6 %slice-start.1 = ((s8[4980736]{0:T(1024)(128)(4,1)}), s8[4194304]{0:T(1024)(128)(4,1)S(1)}, s32[]{:S(2)}) async-start(s8[4980736]{0:T(1024)(128)(4,1)} %bitcast.30), calls=%async_computation.8 | async-start | bytes 8388608
  1159.7 5.3 copy-start.1
Sparse Core Ops, SparseCore 0:
  43.4 208.9 reduce-scatter.2
  255.8 63.6 all-gather.2
  408.7 613.7 reduce-scatter.4
  1025.8 90.1 all-gather.4
where the time goes:
time: 1170 us
  waiting for transfers between devices  848 us (72%)
  blocking collectives  192 us (16%)
  matrix products  53.8 us (5%)
  local copies, waits for them, and re-layouts  34.2 us (3%)
  other arithmetic  28.5 us (2%)
  between operations  15.8 us (1%)
    reduce_scatter x1, waiting for transfers between devices, shards(): lax.psum_scatter(term, ('gx', 'gy'), scatter_dimension=0, tiled=True)  614 us
    reduce_scatter x1, waiting for transfers between devices, shards(): lax.psum_scatter(jnp.dot(block_rows, first_weight, preferred_element_type...  184 us
    psum x2, blocking collectives, shards(): totals, target = lax.psum((row_total, row_target), ('gx', 'gy'))  164 us
    all_gather x1, waiting for transfers between devices, shards(): unit_all = lax.all_gather(unit_half, ('gx', 'gy'), axis=0, tiled=True)  49.6 us
    all_to_all x1, blocking collectives, shards(): lax.all_to_all(features, 'gx', split_axis=1, concat_axis=0, tiled=True)  28.5 us
  transfers between devices with their start and end apart: 4, of which 3 were waited for; matrix products, arithmetic and copies ran while one was open for 6% of the time, Pallas kernels for 0%

commit v1 on v0

v1 whole, which is shorter than its diff:
```python
import functools

import jax
import jax.numpy as jnp
from jax import lax
from jax.experimental import pallas as pl
from jax.experimental.pallas import tpu as pltpu
from jax.sharding import PartitionSpec as P

CLS_DEV = 16128
LOGIT_SCALE = 64.0
COS_MARGIN = 0.4
NORM_EPSILON = 1e-06

MESH = pl.DeviceIdType.MESH
BF16 = jnp.bfloat16
F32 = jnp.float32
IMAGES = 1024
HIDDEN = 768
EMBED = 512
BLOCK = 864
ORDERS = (("x", "y", "z"), ("y", "z", "x"), ("z", "x", "y"))


class Place:
    def __init__(self):
        gx, gy = lax.axis_index("gx"), lax.axis_index("gy")
        self.gx, self.gy = gx, gy
        self.core = lax.rem(gx, 2)
        self.pos = {"y": lax.div(gx, 2), "z": lax.div(gy, 4), "x": lax.rem(gy, 4)}

    def peer(self, axis, d):
        q = lax.rem(self.pos[axis] + d, 4)
        if axis == "y":
            return (q * 2 + self.core, self.gy)
        if axis == "z":
            return (self.gx, q * 4 + self.pos["x"])
        return (self.gx, self.pos["z"] * 4 + q)

    def partner(self):
        return (self.gx + 1 - 2 * self.core, self.gy)

    def row(self, d):
        return (lax.rem(self.gx + d, 8), self.gy)

    def greet(self, whole_row):
        barrier = pltpu.get_barrier_semaphore()
        devices = [self.peer(axis, d) for axis in ("x", "z") for d in (1, 2, 3)]
        if whole_row:
            devices += [self.row(d) for d in range(1, 8)]
        else:
            devices += [self.partner()] + [self.peer("y", d) for d in (1, 2, 3)]
        for device in devices:
            pl.semaphore_signal(barrier, inc=1, device_id=device, device_id_type=MESH)
        pl.semaphore_wait(barrier, len(devices))


def remote(src, dst, send, recv, device):
    return pltpu.make_async_remote_copy(
        src_ref=src, dst_ref=dst, send_sem=send, recv_sem=recv, device_id=device, device_id_type=MESH
    )


def each(count, size, body):
    def step(i, carry):
        body(pl.ds(pl.multiple_of(i * size, size), size))
        return carry

    lax.fori_loop(0, count // size, step, 0)


def sum_scratch(groups):
    return [
        pltpu.VMEM((groups, 1024, 128), F32),
        pltpu.VMEM((groups, 1024, 128), BF16),
        pltpu.VMEM((groups, 1024, 128), BF16),
        pltpu.VMEM((groups, 1024, 128), BF16),
        pltpu.VMEM((groups, 3, 256, 128), BF16),
        pltpu.VMEM((groups, 256, 128), F32),
        pltpu.VMEM((groups, 256, 128), BF16),
        pltpu.VMEM((groups, 3, 64, 128), BF16),
        pltpu.VMEM((groups, 64, 128), F32),
        pltpu.VMEM((groups, 64, 128), BF16),
        pltpu.VMEM((groups, 3, 16, 128), BF16),
        pltpu.SemaphoreType.DMA((groups, 8, 3)),
        pltpu.SemaphoreType.DMA((groups, 8, 3)),
    ]


def sum_everywhere(place, groups, bufs, out):
    acc, s0, r0, s1, r1, acc2, s2, r2, acc3, s3, r3, send, recv = bufs
    core = place.core
    started = []

    def go(src, dst, g, stage, k, device):
        copy = remote(src, dst, send.at[g, stage, k], recv.at[g, stage, k], device)
        copy.start()
        started.append(copy)
        return copy

    def scatter(g, stage, axis, sent, got, size):
        p = place.pos[axis]
        copies = []
        for d in (1, 2, 3):
            q = lax.rem(p + d, 4)
            rows = pl.ds(pl.multiple_of(q * size, size), size)
            copies.append(go(sent.at[g, rows], got.at[g, d - 1], g, stage, d - 1, place.peer(axis, d)))
        return copies

    live = [go(s0.at[g], r0.at[g], g, 0, 0, place.partner()) for g in range(groups)]
    nxt = []
    for g in range(groups):
        live[g].wait_recv()

        def add(rows, g=g):
            total = acc[g, rows, :] + r0[g, rows, :].astype(F32)
            acc[g, rows, :] = total
            s1[g, rows, :] = total.astype(BF16)

        each(1024, 128, add)
        nxt.append(scatter(g, 1, ORDERS[g][0], s1, r1, 256))
    live, nxt = nxt, []
    for g in range(groups):
        for copy in live[g]:
            copy.wait_recv()
        base = place.pos[ORDERS[g][0]] * 256

        def add(rows, g=g, base=base):
            own = pl.ds(pl.multiple_of(base + rows.start, 64), 64)
            total = acc[g, own, :] + (
                r1[g, 0, rows, :].astype(F32) + r1[g, 1, rows, :].astype(F32) + r1[g, 2, rows, :].astype(F32)
            )
            acc2[g, rows, :] = total
            s2[g, rows, :] = total.astype(BF16)

        each(256, 64, add)
        nxt.append(scatter(g, 2, ORDERS[g][1], s2, r2, 64))
    live, nxt = nxt, []
    for g in range(groups):
        for copy in live[g]:
            copy.wait_recv()
        own = pl.ds(pl.multiple_of(place.pos[ORDERS[g][1]] * 64, 64), 64)
        total = acc2[g, own, :] + (r2[g, 0].astype(F32) + r2[g, 1].astype(F32) + r2[g, 2].astype(F32))
        acc3[g] = total
        s3[g] = total.astype(BF16)
        nxt.append(scatter(g, 3, ORDERS[g][2], s3, r3, 16))
    live, nxt = nxt, []

    def spread(g, stage, axis, base, size):
        tile = core * groups + g
        rows = pl.ds(pl.multiple_of(base, size), size)
        part = out.at[tile, rows]
        return [go(part, part, g, stage, d - 1, place.peer(axis, d)) for d in (1, 2, 3)]

    bases = []
    for g in range(groups):
        for copy in live[g]:
            copy.wait_recv()
        p1, p2, p3 = (place.pos[axis] for axis in ORDERS[g])
        bases.append((p1 * 256 + p2 * 64 + p3 * 16, p1 * 256 + p2 * 64, p1 * 256))
        own = pl.ds(pl.multiple_of(p3 * 16, 16), 16)
        total = acc3[g, own, :] + (r3[g, 0].astype(F32) + r3[g, 1].astype(F32) + r3[g, 2].astype(F32))
        out[core * groups + g, pl.ds(pl.multiple_of(bases[g][0], 16), 16), :] = total.astype(BF16)
        nxt.append(spread(g, 4, ORDERS[g][2], bases[g][0], 16))
    for stage, which, size in ((5, 1, 64), (6, 0, 256)):
        live, nxt = nxt, []
        for g in range(groups):
            for copy in live[g]:
                copy.wait_recv()
            nxt.append(spread(g, stage, ORDERS[g][which], bases[g][2 - which], size))
    live, last = nxt, []
    for g in range(groups):
        for copy in live[g]:
            copy.wait_recv()
        whole = out.at[core * groups + g]
        last.append(go(whole, whole, g, 7, 0, place.partner()))
    for copy in last:
        copy.wait_recv()
    for copy in started:
        copy.wait_send()


def project_kernel(features, weight, hidden, blocks, sends, send_sem, recv_sem, *bufs):
    place = Place()
    place.greet(True)
    me = place.gx
    for j in range(8):
        piece = features[:, j * BLOCK : (j + 1) * BLOCK]
        sends[j] = piece
    copies = {}
    for d in (4, 5, 3, 2, 6, 7, 1):
        j = lax.rem(me + d, 8)
        copies[d] = remote(
            sends.at[j],
            blocks.at[pl.ds(pl.multiple_of(me * 128, 128), 128)],
            send_sem.at[d],
            recv_sem.at[d],
            place.row(d),
        )
        copies[d].start()
    blocks[pl.ds(pl.multiple_of(me * 128, 128), 128), :] = sends[me]
    acc, s0 = bufs[0], bufs[1]
    mine = pl.ds(pl.multiple_of(place.core * 384, 128), 384)
    theirs = pl.ds(pl.multiple_of((1 - place.core) * 384, 128), 384)
    for d in range(1, 8):
        copies[d].wait_recv()

    def product(rows):
        block = blocks[rows, :]
        own = jnp.dot(block, weight[:, mine], preferred_element_type=F32)
        other = jnp.dot(block, weight[:, theirs], preferred_element_type=F32)
        for g in range(3):
            acc[g, rows, :] = own[:, g * 128 : (g + 1) * 128]
            s0[g, rows, :] = other[:, g * 128 : (g + 1) * 128].astype(BF16)

    each(1024, 256, product)
    sum_everywhere(place, 3, bufs, hidden)
    for d in range(1, 8):
        copies[d].wait_send()


def project(features, weight):
    return pl.pallas_call(
        project_kernel,
        out_shape=(
            jax.ShapeDtypeStruct((6, IMAGES, 128), BF16),
            jax.ShapeDtypeStruct((IMAGES, BLOCK), BF16),
        ),
        in_specs=[pl.BlockSpec(memory_space=pltpu.VMEM)] * 2,
        out_specs=[pl.BlockSpec(memory_space=pltpu.VMEM)] * 2,
        scratch_shapes=[
            pltpu.VMEM((8, 128, BLOCK), BF16),
            pltpu.SemaphoreType.DMA((8,)),
            pltpu.SemaphoreType.DMA((8,)),
        ]
        + sum_scratch(3),
        compiler_params=pltpu.CompilerParams(collective_id=0, has_side_effects=True),
    )(features, weight)


def embed_kernel(term, out, *bufs):
    place = Place()
    place.greet(False)
    acc, s0 = bufs[0], bufs[1]

    def split(rows):
        for g in range(2):
            mine = pl.ds(pl.multiple_of(place.core * 256 + g * 128, 128), 128)
            theirs = pl.ds(pl.multiple_of((1 - place.core) * 256 + g * 128, 128), 128)
            acc[g, rows, :] = term[rows, mine]
            s0[g, rows, :] = term[rows, theirs].astype(BF16)

    each(1024, 128, split)
    sum_everywhere(place, 2, bufs, out)


def embed_sum(term):
    return pl.pallas_call(
        embed_kernel,
        out_shape=jax.ShapeDtypeStruct((4, IMAGES, 128), BF16),
        in_specs=[pl.BlockSpec(memory_space=pltpu.VMEM)],
        out_specs=pl.BlockSpec(memory_space=pltpu.VMEM),
        scratch_shapes=sum_scratch(2),
        compiler_params=pltpu.CompilerParams(collective_id=1, has_side_effects=True),
    )(term)


def pair_sums(place, value, got, send, recv):
    started = []
    for stage, axis in enumerate(("core", "x", "y", "z")):
        p = place.core if axis == "core" else place.pos[axis]
        got[stage, p] = value
        copies = []
        for d in (1,) if axis == "core" else (1, 2, 3):
            device = place.partner() if axis == "core" else place.peer(axis, d)
            slot = got.at[stage, p]
            copies.append(remote(slot, slot, send.at[stage, d - 1], recv.at[stage, d - 1], device))
            copies[-1].start()
        for copy in copies:
            copy.wait_recv()
        started += copies
        value = got[stage, 0] + got[stage, 1]
        if axis != "core":
            value = value + (got[stage, 2] + got[stage, 3])
    for copy in started:
        copy.wait_send()
    return value


def totals_kernel(pair, out, got, send, recv):
    place = Place()
    place.greet(False)
    out[...] = pair_sums(place, pair[...], got, send, recv)


def totals_sum(pair):
    return pl.pallas_call(
        totals_kernel,
        out_shape=jax.ShapeDtypeStruct((2, IMAGES), F32),
        in_specs=[pl.BlockSpec(memory_space=pltpu.VMEM)],
        out_specs=pl.BlockSpec(memory_space=pltpu.VMEM),
        scratch_shapes=[
            pltpu.VMEM((4, 4, 2, IMAGES), F32),
            pltpu.SemaphoreType.DMA((4, 3)),
            pltpu.SemaphoreType.DMA((4, 3)),
        ],
        compiler_params=pltpu.CompilerParams(collective_id=2, has_side_effects=True),
    )(pair)


def shards(features, first_weight, second_weight, centres, active, labels):
    device = lax.axis_index("gx") * lax.axis_size("gy") + lax.axis_index("gy")
    image_count = labels.shape[0]
    hidden_tiles, block_rows = project(features, first_weight)
    hidden = jnp.transpose(hidden_tiles, (1, 0, 2)).reshape(IMAGES, HIDDEN).astype(F32)
    activation, gelu_back = jax.vjp(jax.nn.gelu, hidden)
    act_half = activation.astype(BF16)
    embedding = jnp.dot(act_half, second_weight, preferred_element_type=F32)
    inv_embed = lax.rsqrt(jnp.sum(embedding * embedding, axis=1, keepdims=True) + NORM_EPSILON)
    unit = embedding * inv_embed
    unit_half = unit.astype(BF16)
    cen = centres.astype(F32)
    inv_cen = lax.rsqrt(jnp.sum(cen * cen, axis=1, keepdims=True) + NORM_EPSILON)
    normed = cen * inv_cen
    normed_half = normed.astype(BF16)
    cosine = jnp.dot(unit_half, normed_half.T, preferred_element_type=F32)
    classes = device * CLS_DEV + active
    matches = labels[:, None] == classes[None, :]
    positive = matches.astype(F32)
    logits = LOGIT_SCALE * (cosine - COS_MARGIN * positive)
    exp_terms = jnp.exp(logits - LOGIT_SCALE)
    row_total = jnp.sum(exp_terms, axis=1)
    row_target = jnp.sum(positive * logits, axis=1)
    pair = totals_sum(jnp.stack([row_total, row_target]))
    totals, target = pair[0], pair[1]
    factor = LOGIT_SCALE / image_count
    coeff = (factor * (exp_terms / totals[:, None] - positive)).astype(BF16)
    term = jnp.dot(coeff, normed_half, preferred_element_type=F32)
    grad_tiles = embed_sum(term)
    grad_unit = jnp.transpose(grad_tiles, (1, 0, 2)).reshape(IMAGES, EMBED).astype(F32)
    grad_normed = jnp.dot(coeff.T, unit_half, preferred_element_type=F32)
    grad_cen = inv_cen * (grad_normed - normed * jnp.sum(grad_normed * normed, axis=1, keepdims=True))
    loss = jnp.mean(LOGIT_SCALE + jnp.log(totals) - target)
    grad_embed = inv_embed * (grad_unit - unit * jnp.sum(grad_unit * unit, axis=1, keepdims=True))
    grad_embed_half = grad_embed.astype(BF16)
    grad_second = jnp.dot(act_half.T, grad_embed_half, preferred_element_type=F32)
    grad_act = jnp.dot(grad_embed_half, second_weight.T, preferred_element_type=F32)
    (grad_hidden,) = gelu_back(grad_act)
    grad_first = jnp.dot(block_rows.T, grad_hidden.astype(BF16), preferred_element_type=F32)
    return (loss, grad_first.astype(BF16), grad_second.astype(BF16), grad_cen.astype(BF16))


def solution(mesh):
    placed = (
        P("gx", "gy"),
        P(("gy", "gx"), None),
        P(),
        P(("gx", "gy"), None),
        P(("gx", "gy")),
        P(),
    )
    return jax.shard_map(
        shards,
        mesh=mesh,
        in_specs=placed,
        out_specs=(P(), P(("gy", "gx"), None), P(), P(("gx", "gy"), None)),
        check_vma=False,
    )
```

time: 1170 us -> 231 us (0.20)
  waiting for transfers between devices: 848 us -> 0 us
  blocking collectives: 192 us -> 0 us
  Pallas kernels: 0 us -> 113 us
  between operations: 15.8 us -> 2.57 us
    reduce_scatter x2 -> x0, waiting for transfers between devices: 798 us -> none  [the longest x1 614 us: shards(): lax.psum_scatter(term, ('gx', 'gy'), scatter_dimension=0, tiled=True)]
    psum x2 -> x0, blocking collectives: 164 us -> none  [shards(): totals, target = lax.psum((row_total, row_target), ('gx', 'gy'))]
    pallas_call x0 -> x3, Pallas kernels: none -> 113 us  [the longest x1 65.9 us: project(): pl.pallas_call(project_kernel, out_shape=(jax.ShapeDtypeStruct((6, IMAGES...]
    all_gather x2 -> x0, waiting for transfers between devices: 49.7 us -> none  [the longest x1 49.6 us: shards(): unit_all = lax.all_gather(unit_half, ('gx', 'gy'), axis=0, tiled=True)]
    all_to_all x1 -> x0, blocking collectives: 28.5 us -> none  [shards(): lax.all_to_all(features, 'gx', split_axis=1, concat_axis=0, tiled=True)]
    convert_element_type x5, other arithmetic: 12.4 us -> 26.7 us  [the longest x1 11.3 us: shards(): coeff = (factor * (exp_terms / totals[:, None] - positive)).astype(BF16)]
    dot_general x8 -> x6, matrix products: 53.8 us -> 51.3 us  [the longest x1 14.1 us: shards(): cosine = jnp.dot(unit_half, normed_half.T, preferred_element_type=F32)]
  transfers between devices with their start and end apart: 4 -> 0, of which waited for: 3 -> 0; matrix products, arithmetic and copies ran while one was open for 6% -> 0% of each run, Pallas kernels for 0% -> 0%
where the time goes in v1:
time: 231 us; the launch traced here: 230 us
  Pallas kernels  113 us (49%)
  matrix products  51.3 us (22%)
  other arithmetic  34.3 us (15%)
  local copies, waits for them, and re-layouts  29 us (13%)
  between operations  2.57 us (1%)
    pallas_call x1, Pallas kernels, project(): pl.pallas_call(project_kernel, out_shape=(jax.ShapeDtypeStruct((6, IMAGES...  65.9 us
    pallas_call x1, Pallas kernels, embed_sum(): pl.pallas_call(embed_kernel, out_shape=jax.ShapeDtypeStruct((4, IMAGES, 1...  34.5 us
    unnamed x24, local copies, waits for them, and re-layouts  19 us
    dot_general x1, matrix products, shards(): cosine = jnp.dot(unit_half, normed_half.T, preferred_element_type=F32)  14.1 us
    dot_general x1, matrix products, shards(): grad_normed = jnp.dot(coeff.T, unit_half, preferred_element_type=F32)  12.6 us
    pallas_call x1, Pallas kernels, totals_sum(): pl.pallas_call(totals_kernel, out_shape=jax.ShapeDtypeStruct((2, IMAGES),...  12.3 us
    convert_element_type x1, other arithmetic, shards(): coeff = (factor * (exp_terms / totals[:, None] - positive)).astype(BF16)  11.3 us
    dot_general x1, matrix products, shards(): jnp.dot(block_rows.T, grad_hidden.astype(BF16), preferred_element_type=F32)  8.47 us

profile of v1, /device:TPU:1, one launch (start us, length us, event | category | flops | bytes accessed | tf_op | source)
XLA Modules:
  0.0 229.8 jit_solution(18115034809969023354)
XLA Ops:
  0.6 0.0 copy-start
  0.7 0.8 broadcast_add_fusion
  1.5 7.5 %copy.18 = bf16[4864,512]{0,1:T(8,128)(2,1)} copy(bf16[4864,512]{1,0:T(8,128)(2,1)} %param.9) | data formatting | bytes 9961472 | tf_op args[3]
  9.0 3.4 %fusion.14 = f32[4864]{0:T(1024)S(1)} fusion(bf16[4864,512]{0,1:T(8,128)(2,1)} %copy.18), kind=kLoop, calls=%fused_computation.20 | loop fusion | flops 7466240 | bytes 5000192 | tf_op jit(solution)/shard_map/reduce_sum | solution.py:323
  12.4 65.9 %shard_map.93 = (bf16[6,1024,128]{2,1,0:T(8,128)(2,1)}, bf16[1024,864]{1,0:T(8,128)(2,1)}) custom-call(bf16[128,6912]{1,0:T(8,128)(2,1)} %features.1, bf16[864,768]{1,0:T(8,128)(2,1)} %weight.1), custom_call_target="tpu_custom_call" | custom-call | tf_op jit(solution)/shard_map/pallas_call | solution.py:223
  78.3 3.3 %convert_bitcast_fusion = f32[1024,6,128]{2,0,1:T(8,128)} fusion(bf16[6,1024,128]{2,1,0:T(8,128)(2,1)} %get-tuple-element.6), kind=kLoop, calls=%fused_computation.32 | loop fusion | flops 786432 | bytes 4718592 | tf_op jit(solution)/shard_map/convert_element_type | solution.py:315
  81.6 3.6 %copy.12 = f32[1024,6,128]{0,2,1:T(8,128)} copy(f32[1024,6,128]{2,0,1:T(8,128)} %convert_bitcast_fusion) | data formatting | bytes 6291456 | tf_op jit(solution)/shard_map/convert_element_type | solution.py:315
  85.2 0.0 slice-start
  85.2 3.7 %copy.17 = f32[1024,768]{1,0:T(8,128)} copy(f32[1024,768]{0,1:T(8,128)} %bitcast.29) | data formatting | bytes 6291456 | tf_op jit(solution)/shard_map/convert_element_type | solution.py:315
  88.8 0.0 copy-done
  88.8 0.0 slice-start.1
  88.8 0.0 copy-start.6
  88.8 3.5 %multiply_reduce_fusion = (f32[1024]{0:T(1024)S(1)}, f32[1024,512]{0,1:T(8,128)S(1)}) fusion(bf16[768,512]{1,0:T(8,128)(2,1)S(1)} %copy-done, f32[1024,768]{1,0:T(8,128)} %copy.17), kind=kOutput, calls=%fused_computation.40 | convolution fusion | flops 813431808 | bytes 6033408 | tf_op jit(solution)/shard_map/dot_general | solution.py:318
  92.3 0.0 copy-start.2
  92.4 0.0 slice-done
  92.4 0.0 slice-done.1
  92.4 0.0 copy-done.6
  92.4 14.1 %fusion.6 = (f32[1024]{0:T(1024)S(1)}, f32[1024]{0:T(1024)S(1)}, f32[1024,4864]{1,0:T(8,128)}) fusion(s32[4864]{0:T(1024)S(1)} %broadcast_add_fusion, s32[1024]{0:T(1024)S(1)} %copy-done.6, bf16[4864,512]{0,1:T(8,128)(2,1)S(1)} %bitcast.26, f32[4864]{0:T(1024)S(1)} %add_rsqrt_fusion, f32[1024,512]{0,1:T(8,128)S(1)} %get-tuple-element.21, ...), kind=kOutput, calls=%fused_computation.10 | convolution fusion | flops 5148637184 | bytes 27056128 | tf_op jit(solution)/shard_map/dot_general | solution.py:326
  106.5 0.0 copy-done.2
  106.5 0.6 pad_maximum_fusion.pair
  107.1 12.3 %shard_map.94 = f32[2,1024]{1,0:T(2,128)} custom-call(f32[2,1024]{1,0:T(2,128)} %pad_maximum_fusion.pair), custom_call_target="tpu_custom_call" | custom-call | tf_op jit(solution)/shard_map/pallas_call | solution.py:297
  119.4 0.8 fusion.38
  120.2 0.6 subtract_reduce_fusion
  121.4 11.3 %fusion.5 = bf16[1024,4864]{1,0:T(8,128)(2,1)S(1)} fusion(f32[1024,4864]{1,0:T(8,128)} %get-tuple-element.22, f32[1024]{0:T(1024)S(1)} %bitcast.31, s32[4864]{0:T(1024)S(1)} %broadcast_add_fusion, s32[1024]{0:T(1024)S(1)} %copy-done.6), kind=kLoop, calls=%fused_computation.8 | loop fusion | flops 49807360 | bytes 29912064 | tf_op jit(solution)/shard_map/convert_element_type | solution.py:337
  132.8 0.0 copy-start.1
  132.8 3.8 %copy-done.1 = bf16[1024,4864]{1,0:T(8,128)(2,1)} copy-done((bf16[1024,4864]{1,0:T(8,128)(2,1)}, bf16[1024,4864]{1,0:T(8,128)(2,1)S(1)}, u32[]{:S(2)}) %copy-start.1) | copy-done | bytes 9961496
  136.6 8.4 %fusion.15.term = f32[1024,512]{1,0:T(8,128)} fusion(bf16[1024,4864]{1,0:T(8,128)(2,1)S(1)} %fusion.5, bf16[4864,512]{0,1:T(8,128)(2,1)} %copy.18, f32[4864]{0:T(1024)S(1)} %add_rsqrt_fusion), kind=kOutput, calls=%fused_computation.23 | convolution fusion | flops 5107744768 | bytes 17058816 | tf_op jit(solution)/shard_map/dot_general | solution.py:338
  144.9 34.5 %shard_map.95 = bf16[4,1024,128]{2,1,0:T(8,128)(2,1)} custom-call(f32[1024,512]{1,0:T(8,128)} %fusion.15.term), custom_call_target="tpu_custom_call" | custom-call | tf_op jit(solution)/shard_map/pallas_call | solution.py:258
  179.4 2.7 %convert_bitcast_fusion.1 = f32[1024,4,128]{2,0,1:T(8,128)} fusion(bf16[4,1024,128]{2,1,0:T(8,128)(2,1)} %shard_map.95), kind=kLoop, calls=%fused_computation.39 | loop fusion | flops 524288 | bytes 3145728 | tf_op jit(solution)/shard_map/convert_element_type | solution.py:340
  182.1 1.9 copy.19
  184.0 0.0 copy-start.3
  184.0 2.1 fusion.26
  186.1 0.1 copy-done.3
  186.2 1.5 fusion.28
  187.8 0.0 copy-start.5
  187.8 8.5 %convolution_convert_fusion = bf16[864,768]{1,0:T(8,128)(2,1)} fusion(bf16[1024,864]{1,0:T(8,128)(2,1)} %get-tuple-element.7, f32[1024,768]{1,0:T(8,128)} %copy.17, bf16[1024,512]{0,1:T(8,128)(2,1)} %fusion.28, bf16[768,512]{1,0:T(8,128)(2,1)S(1)} %copy-done), kind=kOutput, calls=%fused_computation.42 | convolution fusion | flops 2180653056 | bytes 8077312 | tf_op jit(solution)/shard_map/dot_general | solution.py:349
  196.2 0.0 copy-done.5
  196.2 0.0 copy-start.4
  196.2 0.0 slice-start.2
  196.2 4.3 %convolution_convert_fusion.1 = bf16[768,512]{1,0:T(8,128)(2,1)} fusion(bf16[1024,512]{0,1:T(8,128)(2,1)S(1)} %copy-done.5, f32[1024,768]{1,0:T(8,128)} %copy.17), kind=kOutput, calls=%fused_computation.43 | convolution fusion | flops 812777472 | bytes 4980736 | tf_op jit(solution)/shard_map/dot_general | solution.py:346
  200.6 0.0 copy-done.4
  200.6 0.0 slice-start.3
  200.6 12.6 %fusion.10 = (f32[4864]{0:T(1024)S(1)}, f32[4864,512]{0,1:T(8,128)}) fusion(bf16[4864,512]{0,1:T(8,128)(2,1)} %copy.18, f32[4864]{0:T(1024)S(1)} %add_rsqrt_fusion, bf16[1024,4864]{1,0:T(8,128)(2,1)} %copy-done.1, f32[1024,512]{0,1:T(8,128)S(1)} %copy-done.4, f32[1024]{0:T(1024)S(1)} %add_rsqrt_fusion.1), kind=kOutput, calls=%fused_computation.16 | convolution fusion | flops 5111278592 | bytes 27043840 | tf_op jit(solution)/shard_map/dot_general | solution.py:341
  213.2 0.0 slice-done.2
  213.2 0.0 slice-done.3
  213.2 7.9 %fusion.13 = bf16[4864,512]{0,1:T(8,128)(2,1)} fusion(f32[4864,512]{0,1:T(8,128)} %get-tuple-element.24, bf16[4864,512]{0,1:T(8,128)(2,1)S(1)} %bitcast.28, f32[4864]{0:T(1024)S(1)} %get-tuple-element.23, f32[4864]{0:T(1024)S(1)} %add_rsqrt_fusion), kind=kLoop, calls=%fused_computation.19 | loop fusion | flops 14942208 | bytes 19961856 | tf_op jit(solution)/shard_map/convert_element_type | solution.py:350
  221.1 7.6 %copy.21 = bf16[4864,512]{1,0:T(8,128)(2,1)} copy(bf16[4864,512]{0,1:T(8,128)(2,1)} %fusion.13) | data formatting | bytes 9961472
  (4 shorter events, 0.0 us)
Async XLA Ops:
  0.6 88.2 %copy-start = (bf16[768,512]{1,0:T(8,128)(2,1)S(1)}, bf16[768,512]{1,0:T(8,128)(2,1)}, u32[]{:S(2)}) copy-start(bf16[768,512]{1,0:T(8,128)(2,1)} %param.8) | copy-start | bytes 2359300
  85.2 7.2 %slice-start = ((s8[4980736]{0:T(1024)(128)(4,1)}), s8[786432]{0:T(1024)(128)(4,1)S(1)}, s32[]{:S(2)}) async-start(s8[4980736]{0:T(1024)(128)(4,1)} %bitcast.25), calls=%async_computation | async-start | bytes 1572864
  88.8 3.6 %slice-start.1 = ((s8[4980736]{0:T(1024)(128)(4,1)}), s8[4194304]{0:T(1024)(128)(4,1)S(1)}, s32[]{:S(2)}) async-start(s8[4980736]{0:T(1024)(128)(4,1)} %bitcast.25), calls=%async_computation.1 | async-start | bytes 8388608
  88.8 3.6 %copy-start.6 = (s32[1024]{0:T(1024)S(1)}, s32[1024]{0:T(1024)}, u32[]{:S(2)}) copy-start(s32[1024]{0:T(1024)} %param.11) | copy-start | bytes 12292
  92.3 14.1 %copy-start.2 = (f32[1024,512]{0,1:T(8,128)}, f32[1024,512]{0,1:T(8,128)S(1)}, u32[]{:S(2)}) copy-start(f32[1024,512]{0,1:T(8,128)S(1)} %get-tuple-element.21) | copy-start | bytes 6291460
  132.8 3.8 %copy-start.1 = (bf16[1024,4864]{1,0:T(8,128)(2,1)}, bf16[1024,4864]{1,0:T(8,128)(2,1)S(1)}, u32[]{:S(2)}) copy-start(bf16[1024,4864]{1,0:T(8,128)(2,1)S(1)} %fusion.5) | copy-start | bytes 29884420
  184.0 2.2 copy-start.3
  187.8 8.5 %copy-start.5 = (bf16[1024,512]{0,1:T(8,128)(2,1)S(1)}, bf16[1024,512]{0,1:T(8,128)(2,1)}, u32[]{:S(2)}) copy-start(bf16[1024,512]{0,1:T(8,128)(2,1)} %fusion.28) | copy-start | bytes 3145732
  196.2 4.3 %copy-start.4 = (f32[1024,512]{0,1:T(8,128)S(1)}, f32[1024,512]{0,1:T(8,128)}, u32[]{:S(2)}) copy-start(f32[1024,512]{0,1:T(8,128)} %copy-done.2) | copy-start | bytes 6291460
  196.2 16.9 %slice-start.2 = ((s8[4980736]{0:T(1024)(128)(4,1)}), s8[4194304]{0:T(1024)(128)(4,1)S(1)}, s32[]{:S(2)}) async-start(s8[4980736]{0:T(1024)(128)(4,1)} %bitcast.27), calls=%async_computation.2 | async-start | bytes 8388608
  200.6 12.6 %slice-start.3 = ((s8[4980736]{0:T(1024)(128)(4,1)}), s8[786432]{0:T(1024)(128)(4,1)S(1)}, s32[]{:S(2)}) async-start(s8[4980736]{0:T(1024)(128)(4,1)} %bitcast.27), calls=%async_computation.3 | async-start | bytes 1572864

commit v2 on v1

v2 whole, which is shorter than its diff:
```python
import jax
import jax.numpy as jnp
from jax import lax
from jax.experimental import pallas as pl
from jax.experimental.pallas import tpu as pltpu
from jax.sharding import PartitionSpec as P

CLS_DEV = 16128
LOGIT_SCALE = 64.0
COS_MARGIN = 0.4
NORM_EPSILON = 1e-06

MESH = pl.DeviceIdType.MESH
BF16 = jnp.bfloat16
F32 = jnp.float32
IMAGES = 1024
HIDDEN = 768
EMBED = 512
BLOCK = 864
CENTRES = 4864
FACTOR = LOGIT_SCALE / IMAGES
LOG2E = 1.4426950408889634
ROOT = 0.7978845608028654
CUBIC = 0.044715
ORDERS = (("x", "y", "z"), ("y", "z", "x"), ("z", "x", "y"))
TILE = 256


class Place:
    def __init__(self):
        gx, gy = lax.axis_index("gx"), lax.axis_index("gy")
        self.gx, self.gy = gx, gy
        self.core = lax.rem(gx, 2)
        self.pos = {"y": lax.div(gx, 2), "z": lax.div(gy, 4), "x": lax.rem(gy, 4)}

    def peer(self, axis, d):
        q = lax.rem(self.pos[axis] + d, 4)
        if axis == "y":
            return (q * 2 + self.core, self.gy)
        if axis == "z":
            return (self.gx, q * 4 + self.pos["x"])
        return (self.gx, self.pos["z"] * 4 + q)

    def partner(self):
        return (self.gx + 1 - 2 * self.core, self.gy)

    def row(self, d):
        return (lax.rem(self.gx + d, 8), self.gy)

    def greet(self):
        barrier = pltpu.get_barrier_semaphore()
        devices = [self.peer(axis, d) for axis in ("x", "z") for d in (1, 2, 3)]
        devices += [self.row(d) for d in range(1, 8)]
        for device in devices:
            pl.semaphore_signal(barrier, inc=1, device_id=device, device_id_type=MESH)
        pl.semaphore_wait(barrier, len(devices))


def remote(src, dst, send, recv, device):
    return pltpu.make_async_remote_copy(
        src_ref=src, dst_ref=dst, send_sem=send, recv_sem=recv, device_id=device, device_id_type=MESH
    )


def block(index, size):
    return pl.ds(pl.multiple_of(index * size, size), size)


def each(count, body, start=0):
    def step(i, carry):
        body(i)
        return carry

    lax.fori_loop(start, start + count, step, 0)


def sum_scratch(groups):
    return [
        pltpu.VMEM((groups, 1024, 128), F32),
        pltpu.VMEM((groups, 1024, 128), BF16),
        pltpu.VMEM((groups, 1024, 128), BF16),
        pltpu.VMEM((groups, 1024, 128), BF16),
        pltpu.VMEM((groups, 3, 256, 128), BF16),
        pltpu.VMEM((groups, 256, 128), F32),
        pltpu.VMEM((groups, 3, 64, 128), F32),
        pltpu.VMEM((groups, 64, 128), F32),
        pltpu.VMEM((groups, 3, 16, 128), F32),
        pltpu.SemaphoreType.DMA((groups, 8, 3)),
        pltpu.SemaphoreType.DMA((groups, 8, 3)),
    ]


def sum_everywhere(place, groups, bufs, out, fill):
    acc, s0, r0, s1, r1, acc2, r2, acc3, r3, send, recv = bufs
    core = place.core
    started = []

    def go(src, dst, g, stage, k, device):
        copy = remote(src, dst, send.at[g, stage, k], recv.at[g, stage, k], device)
        copy.start()
        started.append(copy)
        return copy

    def scatter(g, stage, axis, sent, got, size):
        copies = []
        for d in (1, 2, 3):
            rows = block(lax.rem(place.pos[axis] + d, 4), size)
            copies.append(go(sent.at[g, rows], got.at[g, d - 1], g, stage, d - 1, place.peer(axis, d)))
        return copies

    live = [go(s0.at[g], r0.at[g], g, 0, 0, place.partner()) for g in range(groups)]
    fill(0)
    nxt = []
    for g in range(groups):
        live[g].wait_recv()

        def add(i, g=g):
            rows = block(i, 128)
            total = acc[g, rows, :] + r0[g, rows, :].astype(F32)
            acc[g, rows, :] = total
            s1[g, rows, :] = total.astype(BF16)

        each(8, add)
        nxt.append(scatter(g, 1, ORDERS[g][0], s1, r1, 256))
    live, nxt = nxt, []
    fill(1)
    for g in range(groups):
        for copy in live[g]:
            copy.wait_recv()
        own = block(place.pos[ORDERS[g][0]], 256)
        acc2[g] = acc[g, own, :] + (r1[g, 0].astype(F32) + r1[g, 1].astype(F32) + r1[g, 2].astype(F32))
        nxt.append(scatter(g, 2, ORDERS[g][1], acc2, r2, 64))
    live, nxt = nxt, []
    fill(2)
    for g in range(groups):
        for copy in live[g]:
            copy.wait_recv()
        own = block(place.pos[ORDERS[g][1]], 64)
        acc3[g] = acc2[g, own, :] + (r2[g, 0] + r2[g, 1] + r2[g, 2])
        nxt.append(scatter(g, 3, ORDERS[g][2], acc3, r3, 16))
    live, nxt = nxt, []
    fill(3)

    def spread(g, stage, axis, base, size):
        part = out.at[core * groups + g, pl.ds(pl.multiple_of(base, size), size)]
        return [go(part, part, g, stage, d - 1, place.peer(axis, d)) for d in (1, 2, 3)]

    bases = []
    for g in range(groups):
        for copy in live[g]:
            copy.wait_recv()
        p1, p2, p3 = (place.pos[axis] for axis in ORDERS[g])
        bases.append((p1 * 256 + p2 * 64 + p3 * 16, p1 * 256 + p2 * 64, p1 * 256))
        total = acc3[g, block(p3, 16), :] + (r3[g, 0] + r3[g, 1] + r3[g, 2])
        out[core * groups + g, pl.ds(pl.multiple_of(bases[g][0], 16), 16), :] = total.astype(BF16)
        nxt.append(spread(g, 4, ORDERS[g][2], bases[g][0], 16))
    for stage, which, size in ((5, 1, 64), (6, 0, 256)):
        live, nxt = nxt, []
        fill(stage - 1)
        for g in range(groups):
            for copy in live[g]:
                copy.wait_recv()
            nxt.append(spread(g, stage, ORDERS[g][which], bases[g][2 - which], size))
    live, last = nxt, []
    fill(6)
    for g in range(groups):
        for copy in live[g]:
            copy.wait_recv()
        whole = out.at[core * groups + g]
        last.append(go(whole, whole, g, 7, 0, place.partner()))
    fill(7)
    for copy in last:
        copy.wait_recv()
    return started


def pair_sums(place, value, got, send, recv, fill):
    started = []
    for stage, axis in enumerate(("core", "x", "y", "z")):
        p = place.core if axis == "core" else place.pos[axis]
        got[stage, p] = value
        copies = []
        for d in (1,) if axis == "core" else (1, 2, 3):
            device = place.partner() if axis == "core" else place.peer(axis, d)
            slot = got.at[stage, p]
            copies.append(remote(slot, slot, send.at[stage, d - 1], recv.at[stage, d - 1], device))
            copies[-1].start()
        fill(stage)
        for copy in copies:
            copy.wait_recv()
        started += copies
        value = got[stage, 0] + got[stage, 1]
        if axis != "core":
            value = value + (got[stage, 2] + got[stage, 3])
    return value, started


def gelu_parts(v):
    t = jnp.tanh(ROOT * (v + CUBIC * (v * v * v)))
    return 0.5 * (1.0 + t), t


def step_kernel(
    features_hbm, weight_hbm, second_hbm, centres_hbm, active, labels,
    loss, grad_first, grad_second, grad_centres,
    features, weight, second, centres, sends, blocks, turned, nh, nht, expt,
    hid, act, act_t, slope, unit, uh, inv_embed, gut, gu, ge, gh,
    sums, got, local_sem, out_sem, a2a_send, a2a_recv, pair_send, pair_recv, *bufs,
):
    one, two = bufs[:11], bufs[11:]
    place = Place()
    me = place.gx
    device = me * 16 + place.gy
    loads = [
        pltpu.make_async_copy(src, dst, local_sem.at[i])
        for i, (src, dst) in enumerate(
            ((features_hbm, features), (weight_hbm, weight), (centres_hbm, centres), (second_hbm, second))
        )
    ]
    for load in loads:
        load.start()
    place.greet()
    loads[0].wait()
    for j in range(8):
        sends[j] = features[:, j * BLOCK : (j + 1) * BLOCK]
    copies = {}
    for d in (4, 5, 3, 2, 6, 7, 1):
        copies[d] = remote(
            sends.at[lax.rem(me + d, 8)], blocks.at[block(me, 128)], a2a_send.at[d], a2a_recv.at[d], place.row(d)
        )
        copies[d].start()
    blocks[block(me, 128), :] = sends[me]

    loads[2].wait()

    def normalise(i):
        rows = block(i, 128)
        cen = centres[rows, :].astype(F32)
        normed = cen * lax.rsqrt(jnp.sum(cen * cen, axis=1, keepdims=True) + NORM_EPSILON)
        nh[rows, :] = normed.astype(BF16)
        nht[:, rows] = jnp.transpose(normed).astype(BF16)

    each(CENTRES // 128, normalise)
    loads[1].wait()
    acc, s0 = one[0], one[1]
    mine = pl.ds(pl.multiple_of(place.core * 384, 128), 384)
    theirs = pl.ds(pl.multiple_of((1 - place.core) * 384, 128), 384)
    for d in range(1, 8):
        copies[d].wait_recv()

    def product(i):
        rows = block(i, 256)
        piece = blocks[rows, :]
        own = jnp.dot(piece, weight[:, mine], preferred_element_type=F32)
        other = jnp.dot(piece, weight[:, theirs], preferred_element_type=F32)
        for g in range(3):
            acc[g, rows, :] = own[:, g * 128 : (g + 1) * 128]
            s0[g, rows, :] = other[:, g * 128 : (g + 1) * 128].astype(BF16)

    each(4, product)

    def turn(i):
        rows = block(i, 128)
        for k in range(0, BLOCK, 128):
            top = min(k + 128, BLOCK)
            turned[k:top, rows] = jnp.transpose(blocks[rows, k:top].astype(F32)).astype(BF16)

    def fill_one(stage):
        if stage == 1:
            each(8, turn)

    started = sum_everywhere(place, 3, one, hid, fill_one)
    loads[3].wait()

    def embed(i):
        rows = block(i, 256)
        for k in range(6):
            v = hid[k, rows, :].astype(F32)
            act[rows, k * 128 : (k + 1) * 128] = (v * gelu_parts(v)[0]).astype(BF16)
        emb = jnp.dot(act[rows, :], second[...], preferred_element_type=F32)
        inv = lax.rsqrt(jnp.sum(emb * emb, axis=1, keepdims=True) + NORM_EPSILON)
        inv_embed[rows, :] = inv
        u = emb * inv
        unit[rows, :] = u
        uh[rows, :] = u.astype(BF16)

    each(4, embed)
    sums[...] = jnp.zeros_like(sums)

    def positives(i, imgs):
        parts = []
        for k in range(TILE // 128):
            row = active[i * (TILE // 128) + k] + device * CLS_DEV
            column = jnp.transpose(jnp.broadcast_to(row, (128, 128)))
            parts.append(
                jnp.concatenate(
                    [column == labels[:, imgs + n * 128 : imgs + (n + 1) * 128] for n in range(2)], axis=1
                )
            )
        return jnp.concatenate(parts, axis=0)

    def forward(i):
        rows = block(i, TILE)
        for imgs in range(0, IMAGES, 256):
            cols = slice(imgs, imgs + 256)
            cosine = lax.dot_general(
                nh[rows, :], uh[cols, :], (((1,), (1,)), ((), ())), preferred_element_type=F32
            )
            match = positives(i, imgs)
            scale = LOGIT_SCALE * LOG2E
            shift = jnp.where(match, scale * (1.0 + COS_MARGIN), scale)
            exp_terms = jnp.exp2(scale * cosine - shift)
            hit = jnp.where(match, cosine - COS_MARGIN, 0.0)
            sums[0, :, cols] += jnp.sum(exp_terms.reshape(TILE // 8, 8, 256), axis=0)
            sums[1, :, cols] += jnp.sum(hit.reshape(TILE // 8, 8, 256), axis=0)
            expt[rows, cols] = exp_terms.astype(BF16)

    each(CENTRES // TILE, forward)

    def slopes(i):
        rows = block(i, 128)
        for k in range(6):
            v = hid[k, rows, :].astype(F32)
            half, t = gelu_parts(v)
            inner = ROOT * (1.0 + 3.0 * CUBIC * (v * v))
            slope[rows, k * 128 : (k + 1) * 128] = half + 0.5 * v * ((1.0 - t * t) * inner)
            act_t[k * 128 : (k + 1) * 128, rows] = jnp.transpose(v * half).astype(BF16)

    def fill_pair(stage):
        each(2, slopes, 2 * stage)

    pair = jnp.concatenate(
        [
            jnp.sum(sums[0], axis=0, keepdims=True),
            jnp.sum(sums[1], axis=0, keepdims=True) * LOGIT_SCALE,
        ],
        axis=0,
    )
    pair, more = pair_sums(place, pair, got, pair_send, pair_recv, fill_pair)
    started += more
    totals, target = pair[0:1, :], pair[1:2, :]
    loss[...] = jnp.sum(LOGIT_SCALE + jnp.log(totals) - target, axis=1, keepdims=True) * (1.0 / IMAGES)
    sums[0, 0:1, :] = FACTOR / totals
    gut[...] = jnp.zeros_like(gut)

    def backward(i):
        rows = block(i, TILE)
        for imgs in range(0, IMAGES, 256):
            cols = slice(imgs, imgs + 256)
            match = positives(i, imgs)
            coeff = expt[rows, cols].astype(F32) * sums[0, 0:1, cols] - jnp.where(match, FACTOR, 0.0)
            coeff = coeff.astype(BF16)
            expt[rows, cols] = coeff
            gut[:, cols] += jnp.dot(nht[:, rows], coeff, preferred_element_type=F32)

    each(CENTRES // TILE, backward)
    acc, s0 = two[0], two[1]

    def split(i):
        rows = block(i, 128)
        for g in range(2):
            mine = block(place.core * 2 + g, 128)
            theirs = block((1 - place.core) * 2 + g, 128)
            acc[g, rows, :] = jnp.transpose(gut[mine, rows])
            s0[g, rows, :] = jnp.transpose(gut[theirs, rows]).astype(BF16)

    each(8, split)

    def centre_grad(i):
        rows = block(i, TILE)
        grad_normed = jnp.dot(expt[rows, :], uh[...], preferred_element_type=F32)
        cen = centres[rows, :].astype(F32)
        inv = lax.rsqrt(jnp.sum(cen * cen, axis=1, keepdims=True) + NORM_EPSILON)
        normed = cen * inv
        along = jnp.sum(grad_normed * normed, axis=1, keepdims=True)
        nh[rows, :] = (inv * (grad_normed - normed * along)).astype(BF16)
        pltpu.make_async_copy(nh.at[rows], grad_centres.at[rows], out_sem.at[i]).start()

    share = (3, 5, 3, 2, 2, 2, 2, 0)

    def fill_two(stage):
        if share[stage]:
            each(share[stage], centre_grad, sum(share[:stage]))

    started += sum_everywhere(place, 2, two, gu, fill_two)

    def finish(i):
        rows = block(i, 256)
        g = jnp.concatenate([gu[k, rows, :] for k in range(4)], axis=1).astype(F32)
        u = unit[rows, :]
        along = jnp.sum(g * u, axis=1, keepdims=True)
        grad_embed = (inv_embed[rows, :] * (g - u * along)).astype(BF16)
        ge[rows, :] = grad_embed
        grad_act = lax.dot_general(
            grad_embed, second[...], (((1,), (1,)), ((), ())), preferred_element_type=F32
        )
        gh[rows, :] = (grad_act * slope[rows, :]).astype(BF16)

    each(4, finish)

    def first(i):
        rows = block(i, 288)
        grad_first[rows, :] = jnp.dot(turned[rows, :], gh[...], preferred_element_type=F32).astype(BF16)

    each(3, first)

    def second_grad(i):
        rows = block(i, 256)
        grad_second[rows, :] = jnp.dot(act_t[rows, :], ge[...], preferred_element_type=F32).astype(BF16)

    each(3, second_grad)

    def drain(i):
        rows = block(i, TILE)
        pltpu.make_async_copy(nh.at[rows], grad_centres.at[rows], out_sem.at[i]).wait()

    each(CENTRES // TILE, drain)
    for d in range(1, 8):
        copies[d].wait_send()
    for copy in started:
        copy.wait_send()


def shards(features, first_weight, second_weight, centres, active, labels):
    in_place = pl.BlockSpec(memory_space=pl.ANY)
    near = pl.BlockSpec(memory_space=pltpu.VMEM)
    dma = pltpu.SemaphoreType.DMA
    loss, grad_first, grad_second, grad_centres = pl.pallas_call(
        step_kernel,
        out_shape=(
            jax.ShapeDtypeStruct((1, 1), F32),
            jax.ShapeDtypeStruct((BLOCK, HIDDEN), BF16),
            jax.ShapeDtypeStruct((HIDDEN, EMBED), BF16),
            jax.ShapeDtypeStruct((CENTRES, EMBED), BF16),
        ),
        in_specs=[in_place] * 4 + [near] * 2,
        out_specs=(near, near, near, in_place),
        scratch_shapes=[
            pltpu.VMEM((128, 8 * BLOCK), BF16),
            pltpu.VMEM((BLOCK, HIDDEN), BF16),
            pltpu.VMEM((HIDDEN, EMBED), BF16),
            pltpu.VMEM((CENTRES, EMBED), BF16),
            pltpu.VMEM((8, 128, BLOCK), BF16),
            pltpu.VMEM((IMAGES, BLOCK), BF16),
            pltpu.VMEM((BLOCK, IMAGES), BF16),
            pltpu.VMEM((CENTRES, EMBED), BF16),
            pltpu.VMEM((EMBED, CENTRES), BF16),
            pltpu.VMEM((CENTRES, IMAGES), BF16),
            pltpu.VMEM((6, IMAGES, 128), BF16),
            pltpu.VMEM((IMAGES, HIDDEN), BF16),
            pltpu.VMEM((HIDDEN, IMAGES), BF16),
            pltpu.VMEM((IMAGES, HIDDEN), F32),
            pltpu.VMEM((IMAGES, EMBED), F32),
            pltpu.VMEM((IMAGES, EMBED), BF16),
            pltpu.VMEM((IMAGES, 1), F32),
            pltpu.VMEM((EMBED, IMAGES), F32),
            pltpu.VMEM((4, IMAGES, 128), BF16),
            pltpu.VMEM((IMAGES, EMBED), BF16),
            pltpu.VMEM((IMAGES, HIDDEN), BF16),
            pltpu.VMEM((2, 8, IMAGES), F32),
            pltpu.VMEM((4, 4, 2, IMAGES), F32),
            dma((4,)),
            dma((CENTRES // TILE,)),
            dma((8,)),
            dma((8,)),
            dma((4, 3)),
            dma((4, 3)),
        ]
        + sum_scratch(3)
        + sum_scratch(2),
        compiler_params=pltpu.CompilerParams(
            collective_id=0, has_side_effects=True, vmem_limit_bytes=67043328
        ),
    )(
        features,
        first_weight,
        second_weight,
        centres,
        active.reshape(CENTRES // 128, 1, 128),
        labels.reshape(1, IMAGES),
    )
    return loss.reshape(()), grad_first, grad_second, grad_centres


def solution(mesh):
    placed = (
        P("gx", "gy"),
        P(("gy", "gx"), None),
        P(),
        P(("gx", "gy"), None),
        P(("gx", "gy")),
        P(),
    )
    return jax.shard_map(
        shards,
        mesh=mesh,
        in_specs=placed,
        out_specs=(P(), P(("gy", "gx"), None), P(), P(("gx", "gy"), None)),
        check_vma=False,
    )
```

time: 231 us -> 151 us (0.65)
  matrix products: 51.3 us -> 0 us
  other arithmetic: 34.3 us -> 0 us
  Pallas kernels: 113 us -> 139 us
  local copies, waits for them, and re-layouts: 29 us -> 9.71 us
    dot_general x6 -> x0, matrix products: 51.3 us -> none  [the longest x1 14.1 us: shards(): cosine = jnp.dot(unit_half, normed_half.T, preferred_element_type=F32)]
    convert_element_type x5 -> x0, other arithmetic: 26.7 us -> none  [the longest x1 11.3 us: shards(): coeff = (factor * (exp_terms / totals[:, None] - positive)).astype(BF16)]
    pallas_call x3 -> x1, Pallas kernels: 113 us -> 139 us  [shards(): pl.pallas_call(step_kernel, out_shape=(jax.ShapeDtypeStruct((1, 1), F32),...]
    unnamed x24 -> x5, local copies, waits for them, and re-layouts: 19 us -> 8.36 us
    convert_element_type x3 -> x0, local copies, waits for them, and re-layouts: 9.16 us -> none  [the longest x2 7.24 us: shards(): jnp.transpose(hidden_tiles, (1, 0, 2)).reshape(IMAGES, HIDDEN).astype(F32)]
    reduce_sum x3 -> x0, other arithmetic: 6.14 us -> none  [the longest x1 3.42 us: shards(): jnp.sum(cen * cen, axis=1, keepdims=True) + NORM_EPSILON]
where the time goes in v2:
time: 151 us
  Pallas kernels  139 us (92%)
  local copies, waits for them, and re-layouts  9.71 us (6%)
  between operations  2.54 us (2%)
    pallas_call x1, Pallas kernels, shards(): pl.pallas_call(step_kernel, out_shape=(jax.ShapeDtypeStruct((1, 1), F32),...  139 us
    unnamed x5, local copies, waits for them, and re-layouts  8.36 us

profile of v2, /device:TPU:1, one launch (start us, length us, event | category | flops | bytes accessed | tf_op | source)
XLA Modules:
  0.0 151.1 jit_solution(9117704278162971054)
XLA Ops:
  0.6 1.4 reshape.17.active
  2.0 138.9 %shard_map.93 = (f32[1,1]{1,0:T(1,128)}, bf16[864,768]{1,0:T(8,128)(2,1)}, bf16[768,512]{1,0:T(8,128)(2,1)}, bf16[4864,512]{1,0:T(8,128)(2,1)}) custom-call(bf16[128,6912]{1,0:T(8,128)(2,1)} %features_hbm.1, bf16[864,768]{1,0:T(8,128)(2,1)} %weight_hbm.1, bf16[768,512]{1,0:T(8,128)(2,1)} %second_hbm.1, bf16[4864,512]{1,0:T(8,128)(2,1)} %centres_hbm.1, ...), custom_call_target="tpu_custom_call" | custom-call | tf_op jit(solution)/shard_map/pallas_call | solution.py:428
  140.9 0.0 copy-start
  141.7 2.5 %copy.15 = bf16[864,768]{1,0:T(8,128)(2,1)} copy(bf16[864,768]{1,0:T(8,128)(2,1)} %get-tuple-element.17) | data formatting | bytes 2654208
  144.1 0.0 copy-done
  144.1 0.9 copy.16
  145.0 5.0 %copy.17 = bf16[4864,512]{1,0:T(8,128)(2,1)} copy(bf16[4864,512]{1,0:T(8,128)(2,1)} %get-tuple-element.19) | data formatting | bytes 9961472
Async XLA Ops:
  140.9 3.2 %copy-start = (bf16[768,512]{1,0:T(8,128)(2,1)S(1)}, bf16[768,512]{1,0:T(8,128)(2,1)}, u32[]{:S(2)}) copy-start(bf16[768,512]{1,0:T(8,128)(2,1)} %get-tuple-element.18) | copy-start | bytes 2359300

commit v3 on v2

v3 whole, which is shorter than its diff:
```python
import jax
import jax.numpy as jnp
from jax import lax
from jax.experimental import pallas as pl
from jax.experimental.pallas import tpu as pltpu
from jax.sharding import PartitionSpec as P

CLS_DEV = 16128
LOGIT_SCALE = 64.0
COS_MARGIN = 0.4
NORM_EPSILON = 1e-06

MESH = pl.DeviceIdType.MESH
BF16 = jnp.bfloat16
F32 = jnp.float32
IMAGES = 1024
HIDDEN = 768
EMBED = 512
BLOCK = 864
CENTRES = 4864
FACTOR = LOGIT_SCALE / IMAGES
LOG2E = 1.4426950408889634
ROOT = 0.7978845608028654
CUBIC = 0.044715
ORDERS = (("x", "y", "z"), ("y", "z", "x"), ("z", "x", "y"))
TILE = 256


class Place:
    def __init__(self):
        gx, gy = lax.axis_index("gx"), lax.axis_index("gy")
        self.gx, self.gy = gx, gy
        self.core = lax.rem(gx, 2)
        self.pos = {"y": lax.div(gx, 2), "z": lax.div(gy, 4), "x": lax.rem(gy, 4)}

    def peer(self, axis, d):
        q = lax.rem(self.pos[axis] + d, 4)
        if axis == "y":
            return (q * 2 + self.core, self.gy)
        if axis == "z":
            return (self.gx, q * 4 + self.pos["x"])
        return (self.gx, self.pos["z"] * 4 + q)

    def partner(self):
        return (self.gx + 1 - 2 * self.core, self.gy)

    def row(self, d):
        return (lax.rem(self.gx + d, 8), self.gy)

    def greet(self, meanwhile):
        barrier = pltpu.get_barrier_semaphore()
        devices = [self.peer(axis, d) for axis in ("x", "z") for d in (1, 2, 3)]
        devices += [self.row(d) for d in range(1, 8)]
        for device in devices:
            pl.semaphore_signal(barrier, inc=1, device_id=device, device_id_type=MESH)
        meanwhile()
        pl.semaphore_wait(barrier, len(devices))


def remote(src, dst, send, recv, device):
    return pltpu.make_async_remote_copy(
        src_ref=src, dst_ref=dst, send_sem=send, recv_sem=recv, device_id=device, device_id_type=MESH
    )


def block(index, size):
    return pl.ds(pl.multiple_of(index * size, size), size)


def each(count, body, start=0):
    def step(i, carry):
        body(i)
        return carry

    lax.fori_loop(start, start + count, step, 0)


def sum_scratch(groups):
    return [
        pltpu.VMEM((groups, 512, 128), F32),
        pltpu.VMEM((groups, 512, 128), F32),
        pltpu.VMEM((groups, 512, 128), F32),
        pltpu.VMEM((groups, 512, 128), BF16),
        pltpu.VMEM((groups, 3, 128, 128), BF16),
        pltpu.VMEM((groups, 128, 128), F32),
        pltpu.VMEM((groups, 3, 32, 128), F32),
        pltpu.VMEM((groups, 4, 32, 128), F32),
        pltpu.SemaphoreType.DMA((groups, 7, 3)),
        pltpu.SemaphoreType.DMA((groups, 7, 3)),
    ]


def sum_everywhere(place, half, groups, bufs, out, started):
    acc, s0, r0, s1, r1, acc2, r2, x3, send, recv = bufs
    core = place.core

    def go(src, dst, g, stage, k, device):
        copy = remote(src, dst, send.at[g, stage, k], recv.at[g, stage, k], device)
        copy.start()
        started.append(copy)
        return copy

    def scatter(g, stage, axis, sent, got, size):
        copies = []
        for d in (2, 1, 3):
            rows = block(lax.rem(place.pos[axis] + d, 4), size)
            copies.append(go(sent.at[g, rows], got.at[g, d - 1], g, stage, d - 1, place.peer(axis, d)))
        return copies

    def spread(g, stage, axis, base, size):
        part = out.at[core * groups + g, pl.ds(pl.multiple_of(base, size), size)]
        return [go(part, part, g, stage, d - 1, place.peer(axis, d)) for d in (2, 1, 3)]

    live = [go(s0.at[g], r0.at[g], g, 0, 0, place.partner()) for g in range(groups)]
    yield
    nxt = []
    for g in range(groups):
        live[g].wait_recv()

        def add(i, g=g):
            rows = block(i, 128)
            total = acc[g, rows, :] + r0[g, rows, :]
            acc[g, rows, :] = total
            s1[g, rows, :] = total.astype(BF16)

        each(4, add)
        nxt.append(scatter(g, 1, ORDERS[g][0], s1, r1, 128))
    live, nxt = nxt, []
    yield
    for g in range(groups):
        for copy in live[g]:
            copy.wait_recv()
        own = block(place.pos[ORDERS[g][0]], 128)
        acc2[g] = acc[g, own, :] + (r1[g, 0].astype(F32) + r1[g, 1].astype(F32) + r1[g, 2].astype(F32))
        nxt.append(scatter(g, 2, ORDERS[g][1], acc2, r2, 32))
    live, nxt = nxt, []
    yield
    for g in range(groups):
        for copy in live[g]:
            copy.wait_recv()
        own = block(place.pos[ORDERS[g][1]], 32)
        p = place.pos[ORDERS[g][2]]
        x3[g, p] = acc2[g, own, :] + (r2[g, 0] + r2[g, 1] + r2[g, 2])
        slot = x3.at[g, p]
        nxt.append([go(slot, slot, g, 3, d - 1, place.peer(ORDERS[g][2], d)) for d in (2, 1, 3)])
    live, nxt = nxt, []
    yield
    bases = []
    for g in range(groups):
        for copy in live[g]:
            copy.wait_recv()
        first = half * 512 + place.pos[ORDERS[g][0]] * 128
        bases.append((first + place.pos[ORDERS[g][1]] * 32, first))
        total = (x3[g, 0] + x3[g, 1]) + (x3[g, 2] + x3[g, 3])
        out[core * groups + g, pl.ds(pl.multiple_of(bases[g][0], 32), 32), :] = total.astype(BF16)
        nxt.append(spread(g, 4, ORDERS[g][1], bases[g][0], 32))
    live, nxt = nxt, []
    yield
    for g in range(groups):
        for copy in live[g]:
            copy.wait_recv()
        nxt.append(spread(g, 5, ORDERS[g][0], bases[g][1], 128))
    live, last = nxt, []
    yield
    for g in range(groups):
        for copy in live[g]:
            copy.wait_recv()
        whole = out.at[core * groups + g, pl.ds(half * 512, 512)]
        last.append(go(whole, whole, g, 6, 0, place.partner()))
    yield
    for copy in last:
        copy.wait_recv()


def pair_sums(place, value, got, send, recv, started, keep):
    for stage, axis in enumerate(("core", "x", "y", "z")):
        p = place.core if axis == "core" else place.pos[axis]
        got[stage, p] = value
        copies = []
        for d in (1,) if axis == "core" else (2, 1, 3):
            device = place.partner() if axis == "core" else place.peer(axis, d)
            slot = got.at[stage, p]
            copies.append(remote(slot, slot, send.at[stage, d - 1], recv.at[stage, d - 1], device))
            copies[-1].start()
        yield
        for copy in copies:
            copy.wait_recv()
        started += copies
        value = got[stage, 0] + got[stage, 1]
        if axis != "core":
            value = value + (got[stage, 2] + got[stage, 3])
    keep.append(value)


def gelu_parts(v):
    t = jnp.tanh(ROOT * (v + CUBIC * (v * v * v)))
    return 0.5 * (1.0 + t), t


def step_kernel(
    features_hbm, weight_hbm, second_hbm, centres_hbm, active, labels,
    loss, turned_hbm, gh_hbm, act_t_hbm, ge_hbm, grad_centres,
    features, weight, second, centres, sends, blocks, turned, nh, nht, expt,
    hid, act, act_t, slope, unit, uh, inv_embed, gut, gu, ge,
    sums, got, places, local_sem, out_sem, a2a_send, a2a_recv, pair_send, pair_recv, *bufs,
):
    size = len(bufs) // 4
    one, two = (bufs[:size], bufs[size : 2 * size]), (bufs[2 * size : 3 * size], bufs[3 * size :])
    place = Place()
    me = place.gx
    device = me * 16 + place.gy
    started, leaving = [], []
    loads = [
        pltpu.make_async_copy(src, dst, local_sem.at[i])
        for i, (src, dst) in enumerate(
            ((features_hbm, features), (centres_hbm, centres), (weight_hbm, weight), (second_hbm, second))
        )
    ]

    def leave(src, dst):
        leaving.append(pltpu.make_async_copy(src, dst, local_sem.at[4 + len(leaving)]))
        leaving[-1].start()

    def prepare():
        for load in loads:
            load.start()
        loads[0].wait()
        for j in range(8):
            sends[j] = features[:, j * BLOCK : (j + 1) * BLOCK]

    place.greet(prepare)
    copies = ({}, {})
    for half in range(2):
        for d in (4, 5, 3, 2, 6, 7, 1):
            copies[half][d] = remote(
                sends.at[lax.rem(me + d, 8), pl.ds(half * 64, 64)],
                blocks.at[pl.ds(pl.multiple_of(half * 512 + me * 64, 64), 64)],
                a2a_send.at[half, d],
                a2a_recv.at[half, d],
                place.row(d),
            )
            copies[half][d].start()
    for half in range(2):
        blocks[pl.ds(pl.multiple_of(half * 512 + me * 64, 64), 64), :] = sends[me, half * 64 : half * 64 + 64, :]
        for j in range(8):
            spot = half * 512 + j * 64
            places[:, spot : spot + 64] = labels[:, j * 128 + half * 64 : j * 128 + half * 64 + 64]
    sums[...] = jnp.zeros_like(sums)
    loads[1].wait()

    def normalise(i):
        rows = block(i, 128)
        cen = centres[rows, :].astype(F32)
        normed = cen * lax.rsqrt(jnp.sum(cen * cen, axis=1, keepdims=True) + NORM_EPSILON)
        nh[rows, :] = normed.astype(BF16)
        nht[:, rows] = jnp.transpose(normed).astype(BF16)

    def product(half):
        acc, s0 = one[half][0], one[half][1]
        mine = pl.ds(pl.multiple_of(place.core * 384, 128), 384)
        theirs = pl.ds(pl.multiple_of((1 - place.core) * 384, 128), 384)
        for d in range(1, 8):
            copies[half][d].wait_recv()

        def step(i):
            rows = block(i, 256)
            piece = blocks[pl.ds(pl.multiple_of(half * 512 + i * 256, 256), 256), :]
            other = jnp.dot(piece, weight[:, theirs], preferred_element_type=F32)
            own = jnp.dot(piece, weight[:, mine], preferred_element_type=F32)
            for g in range(3):
                acc[g, rows, :] = own[:, g * 128 : (g + 1) * 128]
                s0[g, rows, :] = other[:, g * 128 : (g + 1) * 128]

        each(2, step)
        return sum_everywhere(place, half, 3, one[half], hid, started)

    def turn(i):
        rows = block(i, 128)
        for k in range(0, BLOCK, 128):
            top = min(k + 128, BLOCK)
            turned[k:top, rows] = jnp.transpose(blocks[rows, k:top].astype(F32)).astype(BF16)

    def embed(i):
        rows = block(i, 256)
        for k in range(6):
            v = hid[k, rows, :].astype(F32)
            act[rows, k * 128 : (k + 1) * 128] = (v * gelu_parts(v)[0]).astype(BF16)
        emb = jnp.dot(act[rows, :], second[...], preferred_element_type=F32)
        inv = lax.rsqrt(jnp.sum(emb * emb, axis=1, keepdims=True) + NORM_EPSILON)
        inv_embed[rows, :] = inv
        u = emb * inv
        unit[rows, :] = u
        uh[rows, :] = u.astype(BF16)

    def columns(i):
        parts = []
        for k in range(TILE // 128):
            row = active[:, block(i * (TILE // 128) + k, 128)] + device * CLS_DEV
            parts.append(jnp.transpose(jnp.broadcast_to(row, (128, 128))))
        return jnp.concatenate(parts, axis=0)

    def matches(column, imgs):
        return jnp.concatenate(
            [column == places[:, imgs + n * 128 : imgs + (n + 1) * 128] for n in range(2)], axis=1
        )

    def forward(half):
        def step(i):
            rows = block(i, TILE)
            column = columns(i)
            for imgs in range(half * 512, half * 512 + 512, 256):
                cols = slice(imgs, imgs + 256)
                cosine = lax.dot_general(
                    nh[rows, :], uh[cols, :], (((1,), (1,)), ((), ())), preferred_element_type=F32
                )
                match = matches(column, imgs)
                scale = LOGIT_SCALE * LOG2E
                shift = jnp.where(match, scale * (1.0 + COS_MARGIN), scale)
                exp_terms = jnp.exp2(scale * cosine - shift)
                hit = jnp.where(match, cosine - COS_MARGIN, 0.0)
                sums[0, :, cols] += jnp.sum(exp_terms.reshape(TILE // 8, 8, 256), axis=0)
                sums[1, :, cols] += jnp.sum(hit.reshape(TILE // 8, 8, 256), axis=0)
                expt[rows, cols] = exp_terms.astype(BF16)

        return step

    def slopes(i):
        rows = block(i, 128)
        for k in range(6):
            v = hid[k, rows, :].astype(F32)
            half, t = gelu_parts(v)
            inner = ROOT * (1.0 + 3.0 * CUBIC * (v * v))
            slope[rows, k * 128 : (k + 1) * 128] = half + 0.5 * v * ((1.0 - t * t) * inner)
            act_t[k * 128 : (k + 1) * 128, rows] = jnp.transpose(v * half).astype(BF16)

    found = ([], [])

    def totals(half):
        cols = slice(half * 512, half * 512 + 512)
        pair = jnp.concatenate(
            [
                jnp.sum(sums[0, :, cols], axis=0, keepdims=True),
                jnp.sum(sums[1, :, cols], axis=0, keepdims=True) * LOGIT_SCALE,
            ],
            axis=0,
        )
        return pair_sums(
            place, pair, got.at[half], pair_send.at[half], pair_recv.at[half], started, found[half]
        )

    def settle(half):
        total, target = found[half][0][0:1, :], found[half][0][1:2, :]
        part = jnp.sum(LOGIT_SCALE + jnp.log(total) - target, axis=1, keepdims=True) * (1.0 / IMAGES)
        loss[...] = part if half == 0 else loss[...] + part
        sums[0, 0:1, half * 512 : half * 512 + 512] = FACTOR / total
        gut[...] = jnp.zeros_like(gut)

    def backward(half):
        def step(i):
            rows = block(i, TILE)
            column = columns(i)
            for part in range(0, 512, 256):
                imgs = half * 512 + part
                cols = slice(imgs, imgs + 256)
                match = matches(column, imgs)
                coeff = expt[rows, cols].astype(F32) * sums[0, 0:1, cols] - jnp.where(match, FACTOR, 0.0)
                coeff = coeff.astype(BF16)
                expt[rows, cols] = coeff
                gut[:, part : part + 256] += jnp.dot(nht[:, rows], coeff, preferred_element_type=F32)

        return step

    def split(half):
        acc, s0 = two[half][0], two[half][1]

        def step(i):
            rows = block(i, 128)
            for g in range(2):
                mine = block(place.core * 2 + g, 128)
                theirs = block((1 - place.core) * 2 + g, 128)
                acc[g, rows, :] = jnp.transpose(gut[mine, rows])
                s0[g, rows, :] = jnp.transpose(gut[theirs, rows])

        each(4, step)
        return sum_everywhere(place, half, 2, two[half], gu, started)

    done = [0]

    def centre_grads(count):
        def step(i):
            rows = block(i, TILE)
            grad_normed = jnp.dot(expt[rows, :], uh[...], preferred_element_type=F32)
            cen = centres[rows, :].astype(F32)
            inv = lax.rsqrt(jnp.sum(cen * cen, axis=1, keepdims=True) + NORM_EPSILON)
            normed = cen * inv
            along = jnp.sum(grad_normed * normed, axis=1, keepdims=True)
            nh[rows, :] = (inv * (grad_normed - normed * along)).astype(BF16)
            pltpu.make_async_copy(nh.at[rows], grad_centres.at[rows], out_sem.at[i]).start()

        each(count, step, done[0])
        done[0] += count

    def finish(half):
        def step(i):
            rows = block(i, 256)
            g = jnp.concatenate([gu[k, rows, :] for k in range(4)], axis=1).astype(F32)
            u = unit[rows, :]
            along = jnp.sum(g * u, axis=1, keepdims=True)
            grad_embed = (inv_embed[rows, :] * (g - u * along)).astype(BF16)
            ge[rows, :] = grad_embed
            grad_act = lax.dot_general(
                grad_embed, second[...], (((1,), (1,)), ((), ())), preferred_element_type=F32
            )
            act[rows, :] = (grad_act * slope[rows, :]).astype(BF16)

        each(2, step, 2 * half)
        rows = pl.ds(half * 512, 512)
        leave(act.at[rows], gh_hbm.at[rows])
        leave(ge.at[rows], ge_hbm.at[rows])

    def go(steps):
        next(steps, None)

    each(CENTRES // 128, normalise)
    loads[2].wait()
    a1 = product(0)
    go(a1)
    each(4, turn)
    go(a1)
    go(a1)
    go(a1)
    b1 = product(1)
    go(b1)
    each(4, turn, 4)
    leave(turned, turned_hbm)
    go(b1)
    go(a1)
    go(a1)
    go(b1)
    go(a1)
    go(b1)
    loads[3].wait()
    go(a1)
    each(2, embed)
    step = forward(0)
    each(6, step)
    go(b1)
    each(6, step, 6)
    go(b1)
    each(7, step, 12)
    ta = totals(0)
    go(ta)
    go(b1)
    each(2, slopes)
    go(ta)
    go(b1)
    each(2, embed, 2)
    step = forward(1)
    each(6, step)
    go(ta)
    each(6, step, 6)
    go(ta)
    each(7, step, 12)
    tb = totals(1)
    go(tb)
    each(1, slopes, 2)
    go(ta)
    settle(0)
    step = backward(0)
    each(5, step)
    go(tb)
    each(7, step, 5)
    go(tb)
    each(7, step, 12)
    a2 = split(0)
    go(a2)
    each(1, slopes, 3)
    go(tb)
    go(a2)
    each(4, slopes, 4)
    leave(act_t, act_t_hbm)
    go(tb)
    settle(1)
    step = backward(1)
    each(6, step)
    go(a2)
    each(7, step, 6)
    go(a2)
    each(6, step, 13)
    b2 = split(1)
    go(b2)
    go(a2)
    centre_grads(1)
    go(b2)
    centre_grads(4)
    go(a2)
    centre_grads(3)
    go(b2)
    go(a2)
    centre_grads(3)
    go(b2)
    go(a2)
    finish(0)
    centre_grads(2)
    go(b2)
    centre_grads(3)
    go(b2)
    centre_grads(3)
    go(b2)
    go(b2)
    finish(1)
    def drain(i):
        rows = block(i, TILE)
        pltpu.make_async_copy(nh.at[rows], grad_centres.at[rows], out_sem.at[i]).wait()

    each(CENTRES // TILE, drain)
    for copy in leaving:
        copy.wait()
    for half in range(2):
        for d in range(1, 8):
            copies[half][d].wait_send()
    for copy in started:
        copy.wait_send()


def last_kernel(
    turned_hbm, gh_hbm, act_t_hbm, ge_hbm, centres_hbm, loss_in,
    loss, grad_first, grad_second, grad_centres,
    turned, gh, act_t, ge, held, first, second, sem, in_sem, out_sem,
):
    sources = ((turned_hbm, turned), (gh_hbm, gh), (act_t_hbm, act_t), (ge_hbm, ge))
    loads = [pltpu.make_async_copy(src, dst, sem.at[i]) for i, (src, dst) in enumerate(sources)]
    count = 8
    size = CENTRES // count
    parts = [pl.ds(k * size, size) for k in range(count)]
    arrive = [pltpu.make_async_copy(centres_hbm.at[p], held.at[p], in_sem.at[k]) for k, p in enumerate(parts)]
    depart = [pltpu.make_async_copy(held.at[p], grad_centres.at[p], out_sem.at[k]) for k, p in enumerate(parts)]
    for load in loads[:2] + arrive + loads[2:]:
        load.start()
    loss[...] = loss_in[...]
    loads[0].wait()
    loads[1].wait()
    out = []

    def pass_on(lo, hi):
        for k in range(lo, hi):
            arrive[k].wait()
            depart[k].start()

    for n in range(3):
        rows = pl.ds(n * 288, 288)
        first[rows, :] = jnp.dot(turned[rows, :], gh[...], preferred_element_type=F32).astype(BF16)
        out.append(pltpu.make_async_copy(first.at[rows], grad_first.at[rows], sem.at[4 + n]))
        out[-1].start()
        pass_on(2 * n, 2 * n + 2)
    pass_on(6, 8)
    loads[2].wait()
    loads[3].wait()
    for n in range(3):
        rows = pl.ds(n * 256, 256)
        second[rows, :] = jnp.dot(act_t[rows, :], ge[...], preferred_element_type=F32).astype(BF16)
        out.append(pltpu.make_async_copy(second.at[rows], grad_second.at[rows], sem.at[7 + n]))
        out[-1].start()
    for copy in out + depart:
        copy.wait()


def shards(features, first_weight, second_weight, centres, active, labels):
    in_place = pl.BlockSpec(memory_space=pl.ANY)
    near = pl.BlockSpec(memory_space=pltpu.VMEM)
    dma = pltpu.SemaphoreType.DMA
    loss, turned, gh, act_t, ge, grads = pl.pallas_call(
        step_kernel,
        out_shape=(
            jax.ShapeDtypeStruct((1, 1), F32),
            jax.ShapeDtypeStruct((BLOCK, IMAGES), BF16),
            jax.ShapeDtypeStruct((IMAGES, HIDDEN), BF16),
            jax.ShapeDtypeStruct((HIDDEN, IMAGES), BF16),
            jax.ShapeDtypeStruct((IMAGES, EMBED), BF16),
            jax.ShapeDtypeStruct((CENTRES, EMBED), BF16),
        ),
        in_specs=[in_place] * 4 + [near] * 2,
        out_specs=(near,) + (in_place,) * 5,
        scratch_shapes=[
            pltpu.VMEM((128, 8 * BLOCK), BF16),
            pltpu.VMEM((BLOCK, HIDDEN), BF16),
            pltpu.VMEM((HIDDEN, EMBED), BF16),
            pltpu.VMEM((CENTRES, EMBED), BF16),
            pltpu.VMEM((8, 128, BLOCK), BF16),
            pltpu.VMEM((IMAGES, BLOCK), BF16),
            pltpu.VMEM((BLOCK, IMAGES), BF16),
            pltpu.VMEM((CENTRES, EMBED), BF16),
            pltpu.VMEM((EMBED, CENTRES), BF16),
            pltpu.VMEM((CENTRES, IMAGES), BF16),
            pltpu.VMEM((6, IMAGES, 128), BF16),
            pltpu.VMEM((IMAGES, HIDDEN), BF16),
            pltpu.VMEM((HIDDEN, IMAGES), BF16),
            pltpu.VMEM((IMAGES, HIDDEN), F32),
            pltpu.VMEM((IMAGES, EMBED), F32),
            pltpu.VMEM((IMAGES, EMBED), BF16),
            pltpu.VMEM((IMAGES, 1), F32),
            pltpu.VMEM((EMBED, 512), F32),
            pltpu.VMEM((4, IMAGES, 128), BF16),
            pltpu.VMEM((IMAGES, EMBED), BF16),
            pltpu.VMEM((2, 8, IMAGES), F32),
            pltpu.VMEM((2, 4, 4, 2, 512), F32),
            pltpu.VMEM((1, IMAGES), jnp.int32),
            dma((10,)),
            dma((CENTRES // TILE,)),
            dma((2, 8)),
            dma((2, 8)),
            dma((2, 4, 3)),
            dma((2, 4, 3)),
        ]
        + sum_scratch(3) * 2
        + sum_scratch(2) * 2,
        compiler_params=pltpu.CompilerParams(
            collective_id=0, has_side_effects=True, vmem_limit_bytes=67043328
        ),
    )(
        features,
        first_weight,
        second_weight,
        centres,
        active.reshape(1, CENTRES),
        labels.reshape(1, IMAGES),
    )
    loss, grad_first, grad_second, grad_centres = pl.pallas_call(
        last_kernel,
        out_shape=(
            jax.ShapeDtypeStruct((1, 1), F32),
            jax.ShapeDtypeStruct((BLOCK, HIDDEN), BF16),
            jax.ShapeDtypeStruct((HIDDEN, EMBED), BF16),
            jax.ShapeDtypeStruct((CENTRES, EMBED), BF16),
        ),
        in_specs=[in_place] * 5 + [near],
        out_specs=(near,) + (in_place,) * 3,
        scratch_shapes=[
            pltpu.VMEM((BLOCK, IMAGES), BF16),
            pltpu.VMEM((IMAGES, HIDDEN), BF16),
            pltpu.VMEM((HIDDEN, IMAGES), BF16),
            pltpu.VMEM((IMAGES, EMBED), BF16),
            pltpu.VMEM((CENTRES, EMBED), BF16),
            pltpu.VMEM((BLOCK, HIDDEN), BF16),
            pltpu.VMEM((HIDDEN, EMBED), BF16),
            dma((10,)),
            dma((8,)),
            dma((8,)),
        ],
        compiler_params=pltpu.CompilerParams(vmem_limit_bytes=60000000),
    )(turned, gh, act_t, ge, grads, loss)
    return loss.reshape(()), grad_first, grad_second, grad_centres


def solution(mesh):
    placed = (
        P("gx", "gy"),
        P(("gy", "gx"), None),
        P(),
        P(("gx", "gy"), None),
        P(("gx", "gy")),
        P(),
    )
    return jax.shard_map(
        shards,
        mesh=mesh,
        in_specs=placed,
        out_specs=(P(), P(("gy", "gx"), None), P(), P(("gx", "gy"), None)),
        check_vma=False,
    )
```

time: 151 us -> 133 us (0.88)
  local copies, waits for them, and re-layouts: 9.71 us -> 1.35 us
  Pallas kernels: 139 us -> 131 us
  between operations: 2.54 us -> 0.8 us
    pallas_call x1, Pallas kernels: 139 us -> 122 us  [shards(): pl.pallas_call(step_kernel, out_shape=(jax.ShapeDtypeStruct((1, 1), F32),...]
    pallas_call x0 -> x1, Pallas kernels: none -> 8.68 us  [shards(): pl.pallas_call(last_kernel, out_shape=(jax.ShapeDtypeStruct((1, 1), F32),...]
    unnamed x5 -> x0, local copies, waits for them, and re-layouts: 8.36 us -> none
where the time goes in v3:
time: 133 us
  Pallas kernels  131 us (98%)
  local copies, waits for them, and re-layouts  1.35 us (1%)
    pallas_call x1, Pallas kernels, shards(): pl.pallas_call(step_kernel, out_shape=(jax.ShapeDtypeStruct((1, 1), F32),...  122 us
    pallas_call x1, Pallas kernels, shards(): pl.pallas_call(last_kernel, out_shape=(jax.ShapeDtypeStruct((1, 1), F32),...  8.68 us

profile of v3, /device:TPU:1, one launch (start us, length us, event | category | flops | bytes accessed | tf_op | source)
XLA Modules:
  0.0 133.1 jit_solution(14468341791683499628)
XLA Ops:
  0.6 1.3 %reshape.17.active = s32[1,4864]{1,0:T(1,128)} reshape(s32[4864]{0:T(1024)} %param.10) | data formatting | bytes 38912 | tf_op jit(solution)/shard_map/reshape | solution.py:625
  2.0 122.3 %shard_map.93 = (f32[1,1]{1,0:T(1,128)}, bf16[864,1024]{1,0:T(8,128)(2,1)}, bf16[1024,768]{1,0:T(8,128)(2,1)}, bf16[768,1024]{1,0:T(8,128)(2,1)}, bf16[1024,512]{1,0:T(8,128)(2,1)}, /*index=5*/bf16[4864,512]{1,0:T(8,128)(2,1)}) custom-call(bf16[128,6912]{1,0:T(8,128)(2,1)} %features_hbm.1, bf16[864,768]{1,0:T(8,128)(2,1)} %weight_hbm.1, ...), custom_call_target="tpu_custom_call" | custom-call | tf_op jit(solution)/shard_map/pallas_call | solution.py:572
  124.3 8.7 %shard_map.94 = (f32[1,1]{1,0:T(1,128)}, bf16[864,768]{1,0:T(8,128)(2,1)}, bf16[768,512]{1,0:T(8,128)(2,1)}, bf16[4864,512]{1,0:T(8,128)(2,1)}) custom-call(bf16[864,1024]{1,0:T(8,128)(2,1)} %get-tuple-element.14.turned_hbm, bf16[1024,768]{1,0:T(8,128)(2,1)} %get-tuple-element.15.gh_hbm, bf16[768,1024]{1,0:T(8,128)(2,1)} %get-tuple-element.16.act_t_hbm, ...), custom_call_target="tpu_custom_call" | custom-call | tf_op jit(solution)/shard_map/pallas_call | solution.py:628

commit v4 on v3

--- a/solution.py
+++ b/solution.py
@@ -22,7 +22,10 @@
 LOG2E = 1.4426950408889634
 ROOT = 0.7978845608028654
 CUBIC = 0.044715
-ORDERS = (("x", "y", "z"), ("y", "z", "x"), ("z", "x", "y"))
+ORDERS = (
+    (("x", "z", "y"), ("z", "x", "y"), ("x", "z", "y")),
+    (("x", "y", "z"), ("y", "z", "x"), ("z", "x", "y")),
+)
 TILE = 256
 
 
@@ -90,7 +93,7 @@
     ]
 
 
-def sum_everywhere(place, half, groups, bufs, out, started):
+def sum_everywhere(place, half, groups, orders, bufs, out, started):
     acc, s0, r0, s1, r1, acc2, r2, x3, send, recv = bufs
     core = place.core
 
@@ -124,42 +127,42 @@
             s1[g, rows, :] = total.astype(BF16)
 
         each(4, add)
-        nxt.append(scatter(g, 1, ORDERS[g][0], s1, r1, 128))
+        nxt.append(scatter(g, 1, orders[g][0], s1, r1, 128))
     live, nxt = nxt, []
     yield
     for g in range(groups):
         for copy in live[g]:
             copy.wait_recv()
-        own = block(place.pos[ORDERS[g][0]], 128)
+        own = block(place.pos[orders[g][0]], 128)
         acc2[g] = acc[g, own, :] + (r1[g, 0].astype(F32) + r1[g, 1].astype(F32) + r1[g, 2].astype(F32))
-        nxt.append(scatter(g, 2, ORDERS[g][1], acc2, r2, 32))
+        nxt.append(scatter(g, 2, orders[g][1], acc2, r2, 32))
     live, nxt = nxt, []
     yield
     for g in range(groups):
         for copy in live[g]:
             copy.wait_recv()
-        own = block(place.pos[ORDERS[g][1]], 32)
-        p = place.pos[ORDERS[g][2]]
+        own = block(place.pos[orders[g][1]], 32)
+        p = place.pos[orders[g][2]]
         x3[g, p] = acc2[g, own, :] + (r2[g, 0] + r2[g, 1] + r2[g, 2])
         slot = x3.at[g, p]
-        nxt.append([go(slot, slot, g, 3, d - 1, place.peer(ORDERS[g][2], d)) for d in (2, 1, 3)])
+        nxt.append([go(slot, slot, g, 3, d - 1, place.peer(orders[g][2], d)) for d in (2, 1, 3)])
     live, nxt = nxt, []
     yield
     bases = []
     for g in range(groups):
         for copy in live[g]:
             copy.wait_recv()
-        first = half * 512 + place.pos[ORDERS[g][0]] * 128
-        bases.append((first + place.pos[ORDERS[g][1]] * 32, first))
+        first = half * 512 + place.pos[orders[g][0]] * 128
+        bases.append((first + place.pos[orders[g][1]] * 32, first))
         total = (x3[g, 0] + x3[g, 1]) + (x3[g, 2] + x3[g, 3])
         out[core * groups + g, pl.ds(pl.multiple_of(bases[g][0], 32), 32), :] = total.astype(BF16)
-        nxt.append(spread(g, 4, ORDERS[g][1], bases[g][0], 32))
+        nxt.append(spread(g, 4, orders[g][1], bases[g][0], 32))
     live, nxt = nxt, []
     yield
     for g in range(groups):
         for copy in live[g]:
             copy.wait_recv()
-        nxt.append(spread(g, 5, ORDERS[g][0], bases[g][1], 128))
+        nxt.append(spread(g, 5, orders[g][0], bases[g][1], 128))
     live, last = nxt, []
     yield
     for g in range(groups):
@@ -202,7 +205,7 @@
     loss, turned_hbm, gh_hbm, act_t_hbm, ge_hbm, grad_centres,
     features, weight, second, centres, sends, blocks, turned, nh, nht, expt,
     hid, act, act_t, slope, unit, uh, inv_embed, gut, gu, ge,
-    sums, got, places, local_sem, out_sem, a2a_send, a2a_recv, pair_send, pair_recv, *bufs,
+    sums, got, places, held0, held1, pair0, pair1, local_sem, out_sem, a2a_send, a2a_recv, pair_send, pair_recv, *bufs,
 ):
     size = len(bufs) // 4
     one, two = (bufs[:size], bufs[size : 2 * size]), (bufs[2 * size : 3 * size], bufs[3 * size :])
@@ -230,7 +233,7 @@
 
     place.greet(prepare)
     copies = ({}, {})
-    for half in range(2):
+    def exchange(half):
         for d in (4, 5, 3, 2, 6, 7, 1):
             copies[half][d] = remote(
                 sends.at[lax.rem(me + d, 8), pl.ds(half * 64, 64)],
@@ -240,6 +243,8 @@
                 place.row(d),
             )
             copies[half][d].start()
+
+    exchange(0)
     for half in range(2):
         blocks[pl.ds(pl.multiple_of(half * 512 + me * 64, 64), 64), :] = sends[me, half * 64 : half * 64 + 64, :]
         for j in range(8):
@@ -272,7 +277,7 @@
                 s0[g, rows, :] = other[:, g * 128 : (g + 1) * 128]
 
         each(2, step)
-        return sum_everywhere(place, half, 3, one[half], hid, started)
+        return sum_everywhere(place, half, 3, ORDERS[half], one[half], hid, started)
 
     def turn(i):
         rows = block(i, 128)
@@ -299,28 +304,36 @@
             parts.append(jnp.transpose(jnp.broadcast_to(row, (128, 128))))
         return jnp.concatenate(parts, axis=0)
 
-    def matches(column, imgs):
-        return jnp.concatenate(
-            [column == places[:, imgs + n * 128 : imgs + (n + 1) * 128] for n in range(2)], axis=1
+    def cosines(half, i, held):
+        held[...] = lax.dot_general(
+            nh[block(i, TILE), :],
+            uh[half * 512 : half * 512 + 512, :],
+            (((1,), (1,)), ((), ())),
+            preferred_element_type=F32,
         )
 
+    def terms(half, i, held):
+        rows = block(i, TILE)
+        column = columns(i)
+        for part in range(0, 512, 128):
+            cols = slice(half * 512 + part, half * 512 + part + 128)
+            cosine = held[:, part : part + 128]
+            match = column == places[:, cols]
+            scale = LOGIT_SCALE * LOG2E
+            exp_terms = jnp.exp2(scale * cosine - jnp.where(match, scale * (1.0 + COS_MARGIN), scale))
+            hit = jnp.where(match, cosine - COS_MARGIN, 0.0)
+            sums[0, :, cols] += jnp.sum(exp_terms.reshape(TILE // 8, 8, 128), axis=0)
+            sums[1, :, cols] += jnp.sum(hit.reshape(TILE // 8, 8, 128), axis=0)
+            expt[rows, cols] = exp_terms.astype(BF16)
+
     def forward(half):
+        cosines(half, 0, held0)
+
         def step(i):
-            rows = block(i, TILE)
-            column = columns(i)
-            for imgs in range(half * 512, half * 512 + 512, 256):
-                cols = slice(imgs, imgs + 256)
-                cosine = lax.dot_general(
-                    nh[rows, :], uh[cols, :], (((1,), (1,)), ((), ())), preferred_element_type=F32
-                )
-                match = matches(column, imgs)
-                scale = LOGIT_SCALE * LOG2E
-                shift = jnp.where(match, scale * (1.0 + COS_MARGIN), scale)
-                exp_terms = jnp.exp2(scale * cosine - shift)
-                hit = jnp.where(match, cosine - COS_MARGIN, 0.0)
-                sums[0, :, cols] += jnp.sum(exp_terms.reshape(TILE // 8, 8, 256), axis=0)
-                sums[1, :, cols] += jnp.sum(hit.reshape(TILE // 8, 8, 256), axis=0)
-                expt[rows, cols] = exp_terms.astype(BF16)
+            cosines(half, 2 * i + 1, held1)
+            terms(half, 2 * i, held0)
+            cosines(half, 2 * i + 2, held0)
+            terms(half, 2 * i + 1, held1)
 
         return step
 
@@ -355,20 +368,38 @@
         sums[0, 0:1, half * 512 : half * 512 + 512] = FACTOR / total
         gut[...] = jnp.zeros_like(gut)
 
-    def backward(half):
-        def step(i):
+    def coeffs(half, start, held, tiles=2):
+        for k in range(tiles):
+            i = start + k
             rows = block(i, TILE)
             column = columns(i)
-            for part in range(0, 512, 256):
-                imgs = half * 512 + part
-                cols = slice(imgs, imgs + 256)
-                match = matches(column, imgs)
+            for part in range(0, 512, 128):
+                cols = slice(half * 512 + part, half * 512 + part + 128)
+                match = column == places[:, cols]
                 coeff = expt[rows, cols].astype(F32) * sums[0, 0:1, cols] - jnp.where(match, FACTOR, 0.0)
                 coeff = coeff.astype(BF16)
                 expt[rows, cols] = coeff
-                gut[:, part : part + 256] += jnp.dot(nht[:, rows], coeff, preferred_element_type=F32)
+                held[k * TILE : (k + 1) * TILE, part : part + 128] = coeff
+
+    def weigh(start, held, tiles=2):
+        cols = pl.ds(pl.multiple_of(start * TILE, TILE), tiles * TILE)
+        gut[...] += jnp.dot(nht[:, cols], held[: tiles * TILE, :], preferred_element_type=F32)
+
+    def backward(half):
+        coeffs(half, 0, pair0)
+
+        def step(i):
+            weigh(4 * i, pair0)
+            coeffs(half, 4 * i + 2, pair1)
+            weigh(4 * i + 2, pair1)
+            coeffs(half, 4 * i + 4, pair0)
 
         return step
+
+    def backward_end(half):
+        weigh(16, pair0)
+        coeffs(half, 18, pair1, 1)
+        weigh(18, pair1, 1)
 
     def split(half):
         acc, s0 = two[half][0], two[half][1]
@@ -382,23 +413,37 @@
                 s0[g, rows, :] = jnp.transpose(gut[theirs, rows])
 
         each(4, step)
-        return sum_everywhere(place, half, 2, two[half], gu, started)
+        return sum_everywhere(place, half, 2, ORDERS[1], two[half], gu, started)
 
     done = [0]
 
+    def pull(i, held):
+        held[...] = jnp.dot(expt[block(i, TILE), :], uh[...], preferred_element_type=F32)
+
+    def centre(i, held):
+        rows = block(i, TILE)
+        cen = centres[rows, :].astype(F32)
+        inv = lax.rsqrt(jnp.sum(cen * cen, axis=1, keepdims=True) + NORM_EPSILON)
+        normed = cen * inv
+        grad_normed = held[...]
+        along = jnp.sum(grad_normed * normed, axis=1, keepdims=True)
+        nh[rows, :] = (inv * (grad_normed - normed * along)).astype(BF16)
+        pltpu.make_async_copy(nh.at[rows], grad_centres.at[rows], out_sem.at[i]).start()
+
     def centre_grads(count):
+        if done[0] == 0:
+            pull(0, held0)
+
         def step(i):
-            rows = block(i, TILE)
-            grad_normed = jnp.dot(expt[rows, :], uh[...], preferred_element_type=F32)
-            cen = centres[rows, :].astype(F32)
-            inv = lax.rsqrt(jnp.sum(cen * cen, axis=1, keepdims=True) + NORM_EPSILON)
-            normed = cen * inv
-            along = jnp.sum(grad_normed * normed, axis=1, keepdims=True)
-            nh[rows, :] = (inv * (grad_normed - normed * along)).astype(BF16)
-            pltpu.make_async_copy(nh.at[rows], grad_centres.at[rows], out_sem.at[i]).start()
+            pull(2 * i + 1, held1)
+            centre(2 * i, held0)
+            pull(2 * i + 2, held0)
+            centre(2 * i + 1, held1)
 
         each(count, step, done[0])
         done[0] += count
+        if done[0] == 9:
+            centre(18, held0)
 
     def finish(half):
         def step(i):
@@ -421,7 +466,9 @@
     def go(steps):
         next(steps, None)
 
-    each(CENTRES // 128, normalise)
+    each(24, normalise)
+    exchange(1)
+    each(CENTRES // 128 - 24, normalise, 24)
     loads[2].wait()
     a1 = product(0)
     go(a1)
@@ -443,11 +490,12 @@
     go(a1)
     each(2, embed)
     step = forward(0)
-    each(6, step)
+    each(3, step)
     go(b1)
-    each(6, step, 6)
+    each(3, step, 3)
     go(b1)
-    each(7, step, 12)
+    each(3, step, 6)
+    terms(0, 18, held0)
     ta = totals(0)
     go(ta)
     go(b1)
@@ -456,56 +504,55 @@
     go(b1)
     each(2, embed, 2)
     step = forward(1)
-    each(6, step)
+    each(4, step)
     go(ta)
-    each(6, step, 6)
+    each(5, step, 4)
+    terms(1, 18, held0)
     go(ta)
-    each(7, step, 12)
     tb = totals(1)
     go(tb)
-    each(1, slopes, 2)
+    each(2, slopes, 2)
     go(ta)
+    go(tb)
     settle(0)
     step = backward(0)
-    each(5, step)
+    each(2, step)
     go(tb)
-    each(7, step, 5)
-    go(tb)
-    each(7, step, 12)
+    each(2, step, 2)
+    backward_end(0)
     a2 = split(0)
     go(a2)
-    each(1, slopes, 3)
+    each(1, slopes, 4)
     go(tb)
     go(a2)
-    each(4, slopes, 4)
+    each(3, slopes, 5)
     leave(act_t, act_t_hbm)
     go(tb)
     settle(1)
     step = backward(1)
-    each(6, step)
+    each(2, step)
     go(a2)
-    each(7, step, 6)
+    each(2, step, 2)
+    backward_end(1)
     go(a2)
-    each(6, step, 13)
     b2 = split(1)
     go(b2)
-    go(a2)
     centre_grads(1)
     go(b2)
-    centre_grads(4)
     go(a2)
-    centre_grads(3)
+    centre_grads(2)
     go(b2)
     go(a2)
-    centre_grads(3)
+    centre_grads(2)
     go(b2)
     go(a2)
+    go(b2)
+    centre_grads(1)
+    go(a2)
     finish(0)
+    centre_grads(1)
+    go(b2)
     centre_grads(2)
-    go(b2)
-    centre_grads(3)
-    go(b2)
-    centre_grads(3)
     go(b2)
     go(b2)
     finish(1)
@@ -605,6 +652,10 @@
             pltpu.VMEM((2, 8, IMAGES), F32),
             pltpu.VMEM((2, 4, 4, 2, 512), F32),
             pltpu.VMEM((1, IMAGES), jnp.int32),
+            pltpu.VMEM((TILE, 512), F32),
+            pltpu.VMEM((TILE, 512), F32),
+            pltpu.VMEM((2 * TILE, 512), BF16),
+            pltpu.VMEM((2 * TILE, 512), BF16),
             dma((10,)),
             dma((CENTRES // TILE,)),
             dma((2, 8)),

time: 133 us -> 128 us (0.962)
  Pallas kernels: 131 us -> 125 us
    pallas_call x1, Pallas kernels: 122 us -> 117 us  [shards(): pl.pallas_call(step_kernel, out_shape=(jax.ShapeDtypeStruct((1, 1), F32),...]
where the time goes in v4:
time: 128 us
  Pallas kernels  125 us (98%)
  local copies, waits for them, and re-layouts  1.35 us (1%)
    pallas_call x1, Pallas kernels, shards(): pl.pallas_call(step_kernel, out_shape=(jax.ShapeDtypeStruct((1, 1), F32),...  117 us
    pallas_call x1, Pallas kernels, shards(): pl.pallas_call(last_kernel, out_shape=(jax.ShapeDtypeStruct((1, 1), F32),...  8.67 us

profile of v4, /device:TPU:1, one launch (start us, length us, event | category | flops | bytes accessed | tf_op | source)
XLA Modules:
  0.0 127.6 jit_solution(9725194015371155731)
XLA Ops:
  0.6 1.3 %reshape.17.active = s32[1,4864]{1,0:T(1,128)} reshape(s32[4864]{0:T(1024)} %param.10) | data formatting | bytes 38912 | tf_op jit(solution)/shard_map/reshape | solution.py:676
  2.0 116.7 %shard_map.93 = (f32[1,1]{1,0:T(1,128)}, bf16[864,1024]{1,0:T(8,128)(2,1)}, bf16[1024,768]{1,0:T(8,128)(2,1)}, bf16[768,1024]{1,0:T(8,128)(2,1)}, bf16[1024,512]{1,0:T(8,128)(2,1)}, /*index=5*/bf16[4864,512]{1,0:T(8,128)(2,1)}) custom-call(bf16[128,6912]{1,0:T(8,128)(2,1)} %features_hbm.1, bf16[864,768]{1,0:T(8,128)(2,1)} %weight_hbm.1, ...), custom_call_target="tpu_custom_call" | custom-call | tf_op jit(solution)/shard_map/pallas_call | solution.py:619
  118.7 8.7 %shard_map.94 = (f32[1,1]{1,0:T(1,128)}, bf16[864,768]{1,0:T(8,128)(2,1)}, bf16[768,512]{1,0:T(8,128)(2,1)}, bf16[4864,512]{1,0:T(8,128)(2,1)}) custom-call(bf16[864,1024]{1,0:T(8,128)(2,1)} %get-tuple-element.14.turned_hbm, bf16[1024,768]{1,0:T(8,128)(2,1)} %get-tuple-element.15.gh_hbm, bf16[768,1024]{1,0:T(8,128)(2,1)} %get-tuple-element.16.act_t_hbm, ...), custom_call_target="tpu_custom_call" | custom-call | tf_op jit(solution)/shard_map/pallas_call | solution.py:679

commit v5 on v4

v5 whole, which is shorter than its diff:
```python
import jax
import jax.numpy as jnp
import numpy as np
from jax import lax
from jax.experimental import pallas as pl
from jax.experimental.pallas import tpu as pltpu
from jax.sharding import PartitionSpec as P

CLS_DEV = 16128
LOGIT_SCALE = 64.0
COS_MARGIN = 0.4
NORM_EPSILON = 1e-06

MESH = pl.DeviceIdType.MESH
BF16 = jnp.bfloat16
F32 = jnp.float32
IMAGES = 1024
HIDDEN = 768
EMBED = 512
BLOCK = 864
CENTRES = 4864
FACTOR = LOGIT_SCALE / IMAGES
SCALE = float(np.float32(LOGIT_SCALE * 1.4426950408889634))
MARGIN = SCALE * COS_MARGIN
STEP = float(np.float32(SCALE + MARGIN) - np.float32(SCALE))
ROOT = 0.7978845608028654
CUBIC = 0.044715
ORDERS = (
    (("x", "z", "y"), ("z", "x", "y"), ("x", "z", "y")),
    (("x", "y", "z"), ("y", "z", "x"), ("z", "x", "y")),
)
TILE = 256
PARTS = 4
PART = IMAGES // PARTS
SHARE = 128 // PARTS


class Place:
    def __init__(self):
        gx, gy = lax.axis_index("gx"), lax.axis_index("gy")
        self.gx, self.gy = gx, gy
        self.core = lax.rem(gx, 2)
        self.pos = {"y": lax.div(gx, 2), "z": lax.div(gy, 4), "x": lax.rem(gy, 4)}

    def peer(self, axis, d):
        q = lax.rem(self.pos[axis] + d, 4)
        if axis == "y":
            return (q * 2 + self.core, self.gy)
        if axis == "z":
            return (self.gx, q * 4 + self.pos["x"])
        return (self.gx, self.pos["z"] * 4 + q)

    def partner(self):
        return (self.gx + 1 - 2 * self.core, self.gy)

    def row(self, d):
        return (lax.rem(self.gx + d, 8), self.gy)

    def greet(self, meanwhile):
        barrier = pltpu.get_barrier_semaphore()
        devices = [self.peer(axis, d) for axis in ("x", "z") for d in (1, 2, 3)]
        devices += [self.row(d) for d in range(1, 8)]
        for device in devices:
            pl.semaphore_signal(barrier, inc=1, device_id=device, device_id_type=MESH)
        meanwhile()
        pl.semaphore_wait(barrier, len(devices))


def remote(src, dst, send, recv, device):
    return pltpu.make_async_remote_copy(
        src_ref=src, dst_ref=dst, send_sem=send, recv_sem=recv, device_id=device, device_id_type=MESH
    )


def block(index, size):
    return pl.ds(pl.multiple_of(index * size, size), size)


def each(count, body, start=0):
    def step(i, carry):
        body(i)
        return carry

    lax.fori_loop(start, start + count, step, 0)


def sum_scratch(groups):
    return [
        pltpu.VMEM((groups, PART, 128), F32),
        pltpu.VMEM((groups, PART, 128), F32),
        pltpu.VMEM((groups, PART, 128), F32),
        pltpu.VMEM((groups, PART, 128), BF16),
        pltpu.VMEM((groups, 3, PART // 4, 128), BF16),
        pltpu.VMEM((groups, PART // 4, 128), F32),
        pltpu.VMEM((groups, 3, PART // 16, 128), F32),
        pltpu.VMEM((groups, 4, PART // 16, 128), F32),
        pltpu.SemaphoreType.DMA((7,)),
        pltpu.SemaphoreType.DMA((groups, 7)),
    ]


def landed(like, sem):
    pltpu.make_async_copy(like, like, sem).wait()


def sum_everywhere(place, part, groups, orders, bufs, out):
    acc, s0, r0, s1, r1, acc2, r2, x3, send, recv = bufs
    core = place.core
    like = (
        r0,
        r1,
        r2,
        x3.at[:, pl.ds(0, 3)],
        s1.at[:, pl.ds(0, 3 * (PART // 16))],
        r1,
        s1,
    )

    def go(src, dst, g, stage, device):
        remote(src, dst, send.at[stage], recv.at[g, stage], device).start()

    def scatter(g, stage, axis, sent, got, size):
        for d in (2, 1, 3):
            rows = block(lax.rem(place.pos[axis] + d, 4), size)
            go(sent.at[g, rows], got.at[g, d - 1], g, stage, place.peer(axis, d))

    def spread(g, stage, axis, base, size):
        piece = out.at[core * groups + g, pl.ds(pl.multiple_of(base, size), size)]
        for d in (2, 1, 3):
            go(piece, piece, g, stage, place.peer(axis, d))

    for g in range(groups):
        go(s0.at[g], r0.at[g], g, 0, place.partner())
    yield
    for g in range(groups):
        landed(like[0].at[g], recv.at[g, 0])

        def add(i, g=g):
            rows = block(i, 128)
            total = acc[g, rows, :] + r0[g, rows, :]
            acc[g, rows, :] = total
            s1[g, rows, :] = total.astype(BF16)

        each(2, add)
        scatter(g, 1, orders[g][0], s1, r1, PART // 4)
    landed(like[0], send.at[0])
    yield
    for g in range(groups):
        landed(like[1].at[g], recv.at[g, 1])
        own = block(place.pos[orders[g][0]], PART // 4)
        acc2[g] = acc[g, own, :] + (r1[g, 0].astype(F32) + r1[g, 1].astype(F32) + r1[g, 2].astype(F32))
        scatter(g, 2, orders[g][1], acc2, r2, PART // 16)
    landed(like[1], send.at[1])
    yield
    for g in range(groups):
        landed(like[2].at[g], recv.at[g, 2])
        own = block(place.pos[orders[g][1]], PART // 16)
        p = place.pos[orders[g][2]]
        x3[g, p] = acc2[g, own, :] + (r2[g, 0] + r2[g, 1] + r2[g, 2])
        slot = x3.at[g, p]
        for d in (2, 1, 3):
            go(slot, slot, g, 3, place.peer(orders[g][2], d))
    landed(like[2], send.at[2])
    yield
    bases = []
    for g in range(groups):
        landed(like[3].at[g], recv.at[g, 3])
        first = part * PART + place.pos[orders[g][0]] * (PART // 4)
        bases.append((first + place.pos[orders[g][1]] * (PART // 16), first))
        total = (x3[g, 0] + x3[g, 1]) + (x3[g, 2] + x3[g, 3])
        out[core * groups + g, pl.ds(pl.multiple_of(bases[g][0], PART // 16), PART // 16), :] = total.astype(BF16)
        spread(g, 4, orders[g][1], bases[g][0], PART // 16)
    landed(like[3], send.at[3])
    yield
    for g in range(groups):
        landed(like[4].at[g], recv.at[g, 4])
        spread(g, 5, orders[g][0], bases[g][1], PART // 4)
    landed(like[4], send.at[4])
    yield
    for g in range(groups):
        landed(like[5].at[g], recv.at[g, 5])
        whole = out.at[core * groups + g, pl.ds(part * PART, PART)]
        go(whole, whole, g, 6, place.partner())
    landed(like[5], send.at[5])
    yield
    for g in range(groups):
        landed(like[6].at[g], recv.at[g, 6])
    landed(like[6], send.at[6])


def pair_sums(place, value, got, send, recv, keep):
    for stage, axis in enumerate(("core", "x", "y", "z")):
        p = place.core if axis == "core" else place.pos[axis]
        got[stage, p] = value
        slot = got.at[stage, p]
        steps = (1,) if axis == "core" else (2, 1, 3)
        for d in steps:
            device = place.partner() if axis == "core" else place.peer(axis, d)
            remote(slot, slot, send.at[stage], recv.at[stage], device).start()
        yield
        like = got.at[stage, pl.ds(0, len(steps))]
        landed(like, recv.at[stage])
        value = got[stage, 0] + got[stage, 1]
        if axis != "core":
            value = value + (got[stage, 2] + got[stage, 3])
        landed(like, send.at[stage])
    keep.append(value)


def gelu_parts(v):
    t = jnp.tanh(ROOT * (v + CUBIC * (v * v * v)))
    return 0.5 * (1.0 + t), t


def step_kernel(
    features_hbm, weight_hbm, second_hbm, centres_hbm, active, labels,
    loss, grad_first, grad_second, grad_centres,
    features, weight, second, centres, sends, blocks, turned, nh, nht, expt,
    hid, act, act_t, slope, uh, inv_embed, gu, ge, first,
    sums, got, places, spots, where_found, held0, held1, wide0, wide1, pair0, pair1, local_sem, out_sem, a2a_send, a2a_recv, pair_send, pair_recv, *bufs,
):
    size = len(bufs) // (2 * PARTS)
    sets = [bufs[k * size : (k + 1) * size] for k in range(2 * PARTS)]
    one, two = sets[:PARTS], sets[PARTS:]
    place = Place()
    me = place.gx
    device = me * 16 + place.gy
    gut = held0
    loads = [
        pltpu.make_async_copy(src, dst, local_sem.at[i])
        for i, (src, dst) in enumerate(
            ((features_hbm, features), (centres_hbm, centres), (weight_hbm, weight), (second_hbm, second))
        )
    ]

    def prepare():
        for load in loads:
            load.start()
        loads[0].wait()
        for j in range(8):
            sends[j] = features[:, j * BLOCK : (j + 1) * BLOCK]

    place.greet(prepare)
    def exchange(part):
        for d in (4, 5, 3, 2, 6, 7, 1):
            remote(
                sends.at[lax.rem(me + d, 8), pl.ds(part * SHARE, SHARE)],
                blocks.at[pl.ds(pl.multiple_of(part * PART + me * SHARE, SHARE), SHARE)],
                a2a_send.at[part],
                a2a_recv.at[part],
                place.row(d),
            ).start()

    exchange(0)
    for part in range(PARTS):
        low = part * SHARE
        blocks[pl.ds(pl.multiple_of(part * PART + me * SHARE, SHARE), SHARE), :] = sends[me, low : low + SHARE, :]
        for j in range(8):
            spot = part * PART + j * SHARE
            places[:, spot : spot + SHARE] = labels[:, j * 128 + low : j * 128 + low + SHARE]
    sums[...] = jnp.zeros_like(sums)
    where_found[...] = jnp.full_like(where_found, -1.0)
    loads[1].wait()

    def normalise(i):
        rows = block(i, 128)
        cen = centres[rows, :].astype(F32)
        normed = cen * lax.rsqrt(jnp.sum(cen * cen, axis=1, keepdims=True) + NORM_EPSILON)
        nh[rows, :] = normed.astype(BF16)
        nht[:, rows] = jnp.transpose(normed).astype(BF16)

    def product(part):
        acc, s0 = one[part][0], one[part][1]
        mine = pl.ds(pl.multiple_of(place.core * 384, 128), 384)
        theirs = pl.ds(pl.multiple_of((1 - place.core) * 384, 128), 384)
        landed(blocks.at[pl.ds(0, 7 * SHARE)], a2a_recv.at[part])
        piece = blocks[part * PART : part * PART + PART, :]
        other = jnp.dot(piece, weight[:, theirs], preferred_element_type=F32)
        own = jnp.dot(piece, weight[:, mine], preferred_element_type=F32)
        for g in range(3):
            acc[g] = own[:, g * 128 : (g + 1) * 128]
            s0[g] = other[:, g * 128 : (g + 1) * 128]
        return sum_everywhere(place, part, 3, ORDERS[part // 3], one[part], hid)

    def turn(i):
        rows = block(i, 128)
        for k in range(0, BLOCK, 128):
            top = min(k + 128, BLOCK)
            turned[k:top, rows] = jnp.transpose(blocks[rows, k:top].astype(F32)).astype(BF16)

    def embed(i):
        rows = block(i, 256)
        for k in range(6):
            v = hid[k, rows, :].astype(F32)
            act[rows, k * 128 : (k + 1) * 128] = (v * gelu_parts(v)[0]).astype(BF16)
        emb = jnp.dot(act[rows, :], second[...], preferred_element_type=F32)
        inv = lax.rsqrt(jnp.sum(emb * emb, axis=1, keepdims=True) + NORM_EPSILON)
        inv_embed[rows, :] = inv
        u = emb * inv
        uh[rows, :] = u.astype(BF16)

    def locate(i):
        row = active[:, block(i, 128)] + device * CLS_DEV
        column = jnp.transpose(jnp.broadcast_to(row, (128, 128)))
        here = (lax.broadcasted_iota(jnp.int32, (128, 128), 0) + i * 128).astype(F32)
        for part in range(0, IMAGES, 128):
            cols = slice(part, part + 128)
            hit = jnp.where(column == places[:, cols], here, -1.0)
            best = jnp.max(hit.reshape(16, 8, 128), axis=0)
            where_found[:, cols] = jnp.maximum(where_found[:, cols], best)

    def columns(i):
        parts = []
        for k in range(TILE // 128):
            row = active[:, block(i * (TILE // 128) + k, 128)] + device * CLS_DEV
            parts.append(jnp.transpose(jnp.broadcast_to(row, (128, 128))))
        return jnp.concatenate(parts, axis=0)

    def matches(i, imgs):
        spot = spots[:, imgs : imgs + 128] - i * TILE
        return lax.broadcasted_iota(jnp.int32, (TILE, 128), 0) == spot

    def cosines(part, start, held, tiles=2):
        rows = pl.ds(pl.multiple_of(start * TILE, TILE), tiles * TILE)
        held[: tiles * TILE, :] = lax.dot_general(
            nh[rows, :],
            uh[part * PART : part * PART + PART, :],
            (((1,), (1,)), ((), ())),
            preferred_element_type=F32,
        )

    def terms(part, start, held, tiles=2):
        for k in range(tiles):
            i = start + k
            rows = block(i, TILE)
            for low in range(0, PART, 128):
                cols = slice(part * PART + low, part * PART + low + 128)
                cosine = held[k * TILE : (k + 1) * TILE, low : low + 128]
                shift = jnp.where(matches(i, part * PART + low), SCALE + MARGIN, SCALE)
                exp_terms = jnp.exp2(SCALE * cosine - shift)
                hit = (shift - SCALE) * cosine
                sums[0, :, cols] += jnp.sum(exp_terms.reshape(TILE // 8, 8, 128), axis=0)
                sums[1, :, cols] += jnp.sum(hit.reshape(TILE // 8, 8, 128), axis=0)
                expt[rows, cols] = exp_terms.astype(BF16)

    def forward(part, low, high):
        if low == 0:
            cosines(part, 0, held0)

        def step(i):
            cosines(part, 4 * i + 2, held1)
            terms(part, 4 * i, held0)
            cosines(part, 4 * i + 4, held0)
            terms(part, 4 * i + 2, held1)

        each(high - low, step, low)
        if high == 4:
            cosines(part, 18, held1, 1)
            terms(part, 16, held0)
            terms(part, 18, held1, 1)

    def slopes(i):
        rows = block(i, 128)
        for k in range(6):
            v = hid[k, rows, :].astype(F32)
            part, t = gelu_parts(v)
            inner = ROOT * (1.0 + 3.0 * CUBIC * (v * v))
            slope[rows, k * 128 : (k + 1) * 128] = part + 0.5 * v * ((1.0 - t * t) * inner)
            act_t[k * 128 : (k + 1) * 128, rows] = jnp.transpose(v * part).astype(BF16)

    found = [[] for _ in range(PARTS)]

    def totals(part):
        cols = slice(part * PART, part * PART + PART)
        pair = jnp.concatenate(
            [
                jnp.sum(sums[0, :, cols], axis=0, keepdims=True),
                jnp.sum(sums[1, :, cols], axis=0, keepdims=True) * (LOGIT_SCALE / STEP),
            ],
            axis=0,
        )
        return pair_sums(
            place, pair, got.at[part], pair_send.at[part], pair_recv.at[part], found[part]
        )

    def settle(part):
        total, target = found[part][0][0:1, :], found[part][0][1:2, :]
        target = target - LOGIT_SCALE * COS_MARGIN
        mean = jnp.sum(LOGIT_SCALE + jnp.log(total) - target, axis=1, keepdims=True) * (1.0 / IMAGES)
        loss[...] = mean if part == 0 else loss[...] + mean
        sums[0, 0:1, part * PART : part * PART + PART] = FACTOR / total
        gut[...] = jnp.zeros_like(gut)

    def coeffs(part, start, held, tiles=2):
        for k in range(tiles):
            i = start + k
            rows = block(i, TILE)
            column = columns(i)
            for low in range(0, PART, 128):
                cols = slice(part * PART + low, part * PART + low + 128)
                picked = jnp.where(column == places[:, cols], FACTOR, 0.0)
                coeff = expt[rows, cols].astype(F32) * sums[0, 0:1, cols] - picked
                coeff = coeff.astype(BF16)
                expt[rows, cols] = coeff
                held[k * TILE : (k + 1) * TILE, low : low + 128] = coeff

    def weigh(start, held, tiles=2):
        cols = pl.ds(pl.multiple_of(start * TILE, TILE), tiles * TILE)
        gut[...] += jnp.dot(nht[:, cols], held[: tiles * TILE, :], preferred_element_type=F32)

    def backward(part, low, high):
        if low == 0:
            settle(part)
            coeffs(part, 0, pair0)

        def step(i):
            weigh(4 * i, pair0)
            coeffs(part, 4 * i + 2, pair1)
            weigh(4 * i + 2, pair1)
            coeffs(part, 4 * i + 4, pair0)

        each(high - low, step, low)
        if high == 4:
            weigh(16, pair0)
            coeffs(part, 18, pair1, 1)
            weigh(18, pair1, 1)

    def split(part):
        acc, s0 = two[part][0], two[part][1]

        def step(i):
            rows = block(i, 128)
            for g in range(2):
                mine = block(place.core * 2 + g, 128)
                theirs = block((1 - place.core) * 2 + g, 128)
                acc[g, rows, :] = jnp.transpose(gut[mine, rows])
                s0[g, rows, :] = jnp.transpose(gut[theirs, rows])

        each(2, step)
        return sum_everywhere(place, part, 2, ORDERS[1], two[part], gu)

    done = [0]

    def pull(i, held):
        held[...] = jnp.dot(expt[block(i, TILE), :], uh[...], preferred_element_type=F32)

    def centre(i, held):
        rows = block(i, TILE)
        cen = centres[rows, :].astype(F32)
        inv = lax.rsqrt(jnp.sum(cen * cen, axis=1, keepdims=True) + NORM_EPSILON)
        normed = cen * inv
        grad_normed = held[...]
        along = jnp.sum(grad_normed * normed, axis=1, keepdims=True)
        nh[rows, :] = (inv * (grad_normed - normed * along)).astype(BF16)
        pltpu.make_async_copy(nh.at[rows], grad_centres.at[rows], out_sem.at[0]).start()

    def centre_grads(count):
        if done[0] == 0:
            pull(0, wide0)

        def step(i):
            pull(2 * i + 1, wide1)
            centre(2 * i, wide0)
            pull(2 * i + 2, wide0)
            centre(2 * i + 1, wide1)

        each(count, step, done[0])
        done[0] += count
        if done[0] == 9:
            centre(18, wide0)

    def finish(part):
        rows = slice(part * PART, part * PART + PART)
        g = jnp.concatenate([gu[k, rows, :] for k in range(4)], axis=1).astype(F32)
        u = uh[rows, :].astype(F32)
        along = jnp.sum(g * u, axis=1, keepdims=True)
        grad_embed = (inv_embed[rows, :] * (g - u * along)).astype(BF16)
        ge[rows, :] = grad_embed
        grad_act = lax.dot_general(
            grad_embed, second[...], (((1,), (1,)), ((), ())), preferred_element_type=F32
        )
        act[rows, :] = (grad_act * slope[rows, :]).astype(BF16)

    def early(_):
        known = slice(0, IMAGES - PART)

        def rows_of_first(i):
            rows = block(i, 288)
            first[rows, :] = jnp.dot(turned[rows, known], act[known, :], preferred_element_type=F32)

        each(3, rows_of_first)

    def late(_):
        new = slice(IMAGES - PART, IMAGES)

        def rows_of_first(i):
            rows = block(i, 288)
            more = jnp.dot(turned[rows, new], act[new, :], preferred_element_type=F32)
            turned[rows, 0:HIDDEN] = (first[rows, :] + more).astype(BF16)

        def rows_of_second(i):
            rows = block(i, 256)
            act_t[rows, 0:EMBED] = jnp.dot(act_t[rows, :], ge[...], preferred_element_type=F32).astype(BF16)

        each(3, rows_of_first)
        leaving = [pltpu.make_async_copy(turned.at[:, pl.ds(0, HIDDEN)], grad_first, local_sem.at[4])]
        leaving[0].start()
        each(3, rows_of_second)
        leaving.append(pltpu.make_async_copy(act_t.at[:, pl.ds(0, EMBED)], grad_second, local_sem.at[5]))
        leaving[1].start()
        return leaving

    def go(steps):
        next(steps, None)

    c, t, r = [None] * PARTS, [None] * PARTS, [None] * PARTS

    def begin(part):
        c[part] = product(part)
        go(c[part])

    def count(part):
        t[part] = totals(part)
        go(t[part])

    def reduce(part):
        r[part] = split(part)
        go(r[part])

    each(24, normalise)
    exchange(1)
    each(CENTRES // 128 - 24, normalise, 24)
    loads[2].wait()
    begin(0)
    each(2, turn)
    go(c[0])
    exchange(2)
    each(19, locate)
    begin(1)
    go(c[0])
    exchange(3)
    each(2, turn, 2)
    go(c[1])
    each(19, locate, 19)
    spots[...] = jnp.max(where_found[...], axis=0, keepdims=True).astype(jnp.int32)
    go(c[0])
    begin(2)
    go(c[1])
    each(2, turn, 4)
    go(c[2])
    go(c[0])
    go(c[1])
    go(c[0])
    go(c[2])
    begin(3)
    each(2, turn, 6)
    go(c[1])
    go(c[3])
    loads[3].wait()
    go(c[0])
    go(c[2])
    go(c[0])
    embed(0)
    go(c[1])
    go(c[3])
    forward(0, 0, 2)
    go(c[2])
    forward(0, 2, 4)
    count(0)
    go(c[1])
    go(c[3])
    go(c[1])
    embed(1)
    go(c[2])
    go(t[0])
    forward(1, 0, 2)
    go(c[3])
    forward(1, 2, 4)
    count(1)
    go(t[0])
    go(c[2])
    go(c[2])
    embed(2)
    go(t[1])
    go(c[3])
    forward(2, 0, 2)
    go(t[0])
    forward(2, 2, 4)
    count(2)
    go(c[3])
    go(t[1])
    go(c[3])
    embed(3)
    go(t[2])
    forward(3, 0, 2)
    go(t[0])
    go(t[1])
    forward(3, 2, 4)
    count(3)
    go(t[2])
    backward(0, 0, 2)
    go(t[3])
    go(t[1])
    backward(0, 2, 4)
    reduce(0)
    go(t[2])
    backward(1, 0, 2)
    go(r[0])
    go(t[3])
    backward(1, 2, 4)
    reduce(1)
    go(t[2])
    each(2, slopes)
    go(r[1])
    backward(2, 0, 2)
    go(r[0])
    go(t[3])
    backward(2, 2, 4)
    reduce(2)
    go(r[1])
    each(2, slopes, 2)
    go(r[0])
    go(r[2])
    each(2, slopes, 4)
    go(t[3])
    backward(3, 0, 2)
    go(r[1])
    go(r[0])
    go(r[2])
    backward(3, 2, 4)
    reduce(3)
    each(2, slopes, 6)
    go(r[0])
    go(r[3])
    go(r[1])
    go(r[2])
    centre_grads(2)
    go(r[0])
    go(r[1])
    go(r[0])
    go(r[2])
    finish(0)
    go(r[3])
    centre_grads(1)
    go(r[1])
    go(r[2])
    centre_grads(1)
    go(r[1])
    go(r[3])
    finish(1)
    centre_grads(1)
    go(r[2])
    go(r[3])
    go(r[2])
    finish(2)
    centre_grads(1)
    early(0)
    go(r[3])
    centre_grads(2)
    go(r[3])
    centre_grads(1)
    go(r[3])
    finish(3)
    leaving = late(0)

    for part in range(PARTS):
        landed(blocks.at[pl.ds(0, 7 * SHARE)], a2a_send.at[part])
    for copy in leaving:
        copy.wait()
    landed(nh, out_sem.at[0])


def last_kernel(
    first_hbm, second_hbm, centres_hbm, loss_in,
    loss, grad_first, grad_second, grad_centres,
    first, second, held, in_sem, out_sem,
):
    parts = [pl.ds(k * (CENTRES // 8), CENTRES // 8) for k in range(8)]
    ways = [(centres_hbm.at[p], held.at[p], grad_centres.at[p]) for p in parts]
    ways += [(first_hbm, first, grad_first), (second_hbm, second, grad_second)]
    arrive = [pltpu.make_async_copy(w[0], w[1], in_sem.at[k]) for k, w in enumerate(ways)]
    depart = [pltpu.make_async_copy(w[1], w[2], out_sem.at[k]) for k, w in enumerate(ways)]
    for copy in arrive:
        copy.start()
    loss[...] = loss_in[...]
    for there, back in zip(arrive, depart):
        there.wait()
        back.start()
    for copy in depart:
        copy.wait()


def shards(features, first_weight, second_weight, centres, active, labels):
    in_place = pl.BlockSpec(memory_space=pl.ANY)
    near = pl.BlockSpec(memory_space=pltpu.VMEM)
    dma = pltpu.SemaphoreType.DMA
    loss, first, second, grads = pl.pallas_call(
        step_kernel,
        out_shape=(
            jax.ShapeDtypeStruct((1, 1), F32),
            jax.ShapeDtypeStruct((BLOCK, HIDDEN), BF16),
            jax.ShapeDtypeStruct((HIDDEN, EMBED), BF16),
            jax.ShapeDtypeStruct((CENTRES, EMBED), BF16),
        ),
        in_specs=[in_place] * 4 + [near] * 2,
        out_specs=(near,) + (in_place,) * 3,
        scratch_shapes=[
            pltpu.VMEM((128, 8 * BLOCK), BF16),
            pltpu.VMEM((BLOCK, HIDDEN), BF16),
            pltpu.VMEM((HIDDEN, EMBED), BF16),
            pltpu.VMEM((CENTRES, EMBED), BF16),
            pltpu.VMEM((8, 128, BLOCK), BF16),
            pltpu.VMEM((IMAGES, BLOCK), BF16),
            pltpu.VMEM((BLOCK, IMAGES), BF16),
            pltpu.VMEM((CENTRES, EMBED), BF16),
            pltpu.VMEM((EMBED, CENTRES), BF16),
            pltpu.VMEM((CENTRES, IMAGES), BF16),
            pltpu.VMEM((6, IMAGES, 128), BF16),
            pltpu.VMEM((IMAGES, HIDDEN), BF16),
            pltpu.VMEM((HIDDEN, IMAGES), BF16),
            pltpu.VMEM((IMAGES, HIDDEN), F32),
            pltpu.VMEM((IMAGES, EMBED), BF16),
            pltpu.VMEM((IMAGES, 1), F32),
            pltpu.VMEM((4, IMAGES, 128), BF16),
            pltpu.VMEM((IMAGES, EMBED), BF16),
            pltpu.VMEM((BLOCK, HIDDEN), F32),
            pltpu.VMEM((2, 8, IMAGES), F32),
            pltpu.VMEM((PARTS, 4, 4, 2, PART), F32),
            pltpu.VMEM((1, IMAGES), jnp.int32),
            pltpu.VMEM((1, IMAGES), jnp.int32),
            pltpu.VMEM((8, IMAGES), F32),
            pltpu.VMEM((2 * TILE, PART), F32),
            pltpu.VMEM((2 * TILE, PART), F32),
            pltpu.VMEM((TILE, EMBED), F32),
            pltpu.VMEM((TILE, EMBED), F32),
            pltpu.VMEM((2 * TILE, PART), BF16),
            pltpu.VMEM((2 * TILE, PART), BF16),
            dma((6,)),
            dma((1,)),
            dma((PARTS,)),
            dma((PARTS,)),
            dma((PARTS, 4)),
            dma((PARTS, 4)),
        ]
        + sum_scratch(3) * PARTS
        + sum_scratch(2) * PARTS,
        compiler_params=pltpu.CompilerParams(
            collective_id=0, has_side_effects=True, vmem_limit_bytes=67043328
        ),
    )(
        features,
        first_weight,
        second_weight,
        centres,
        active.reshape(1, CENTRES),
        labels.reshape(1, IMAGES),
    )
    loss, grad_first, grad_second, grad_centres = pl.pallas_call(
        last_kernel,
        out_shape=(
            jax.ShapeDtypeStruct((1, 1), F32),
            jax.ShapeDtypeStruct((BLOCK, HIDDEN), BF16),
            jax.ShapeDtypeStruct((HIDDEN, EMBED), BF16),
            jax.ShapeDtypeStruct((CENTRES, EMBED), BF16),
        ),
        in_specs=[in_place] * 3 + [near],
        out_specs=(near,) + (in_place,) * 3,
        scratch_shapes=[
            pltpu.VMEM((BLOCK, HIDDEN), BF16),
            pltpu.VMEM((HIDDEN, EMBED), BF16),
            pltpu.VMEM((CENTRES, EMBED), BF16),
            dma((10,)),
            dma((10,)),
        ],
        compiler_params=pltpu.CompilerParams(vmem_limit_bytes=60000000),
    )(first, second, grads, loss)
    return loss.reshape(()), grad_first, grad_second, grad_centres


def solution(mesh):
    placed = (
        P("gx", "gy"),
        P(("gy", "gx"), None),
        P(),
        P(("gx", "gy"), None),
        P(("gx", "gy")),
        P(),
    )
    return jax.shard_map(
        shards,
        mesh=mesh,
        in_specs=placed,
        out_specs=(P(), P(("gy", "gx"), None), P(), P(("gx", "gy"), None)),
        check_vma=False,
    )
```

time: 128 us -> 119 us (0.930)
  Pallas kernels: 125 us -> 116 us
    pallas_call x1, Pallas kernels: 117 us -> 109 us  [shards(): pl.pallas_call(step_kernel, out_shape=(jax.ShapeDtypeStruct((1, 1), F32),...]
    pallas_call x1, Pallas kernels: 8.67 us -> 7.16 us  [shards(): pl.pallas_call(last_kernel, out_shape=(jax.ShapeDtypeStruct((1, 1), F32),...]
where the time goes in v5:
time: 119 us
  Pallas kernels  116 us (97%)
  local copies, waits for them, and re-layouts  1.35 us (1%)
    pallas_call x1, Pallas kernels, shards(): pl.pallas_call(step_kernel, out_shape=(jax.ShapeDtypeStruct((1, 1), F32),...  109 us
    pallas_call x1, Pallas kernels, shards(): pl.pallas_call(last_kernel, out_shape=(jax.ShapeDtypeStruct((1, 1), F32),...  7.16 us

profile of v5, /device:TPU:1, one launch (start us, length us, event | category | flops | bytes accessed | tf_op | source)
XLA Modules:
  0.0 118.6 jit_solution(1750762712836634287)
XLA Ops:
  0.6 1.3 %reshape.17.active = s32[1,4864]{1,0:T(1,128)} reshape(s32[4864]{0:T(1024)} %param.10) | data formatting | bytes 38912 | tf_op jit(solution)/shard_map/reshape | solution.py:755
  2.0 109.3 %shard_map.93 = (f32[1,1]{1,0:T(1,128)}, bf16[864,768]{1,0:T(8,128)(2,1)}, bf16[768,512]{1,0:T(8,128)(2,1)}, bf16[4864,512]{1,0:T(8,128)(2,1)}) custom-call(bf16[128,6912]{1,0:T(8,128)(2,1)} %features_hbm.1, bf16[864,768]{1,0:T(8,128)(2,1)} %weight_hbm.1, bf16[768,512]{1,0:T(8,128)(2,1)} %second_hbm.1, bf16[4864,512]{1,0:T(8,128)(2,1)} %centres_hbm.1, ...), custom_call_target="tpu_custom_call" | custom-call | tf_op jit(solution)/shard_map/pallas_call | solution.py:697
  111.3 7.2 %shard_map.94 = (f32[1,1]{1,0:T(1,128)}, bf16[864,768]{1,0:T(8,128)(2,1)}, bf16[768,512]{1,0:T(8,128)(2,1)}, bf16[4864,512]{1,0:T(8,128)(2,1)}) custom-call(bf16[864,768]{1,0:T(8,128)(2,1)} %get-tuple-element.12.first_hbm, bf16[768,512]{1,0:T(8,128)(2,1)} %get-tuple-element.13.second_hbm, bf16[4864,512]{1,0:T(8,128)(2,1)} %get-tuple-element.14.centres_hbm, ...), custom_call_target="tpu_custom_call" | custom-call | tf_op jit(solution)/shard_map/pallas_call | solution.py:758

commit v6 on v5

--- a/solution.py
+++ b/solution.py
@@ -26,7 +26,7 @@
 ROOT = 0.7978845608028654
 CUBIC = 0.044715
 ORDERS = (
-    (("x", "z", "y"), ("z", "x", "y"), ("x", "z", "y")),
+    (("u", "v", "y"), ("v", "u", "y"), ("u", "v", "y")),
     (("x", "y", "z"), ("y", "z", "x"), ("z", "x", "y")),
 )
 TILE = 256
@@ -40,12 +40,18 @@
         gx, gy = lax.axis_index("gx"), lax.axis_index("gy")
         self.gx, self.gy = gx, gy
         self.core = lax.rem(gx, 2)
-        self.pos = {"y": lax.div(gx, 2), "z": lax.div(gy, 4), "x": lax.rem(gy, 4)}
+        x, z = lax.rem(gy, 4), lax.div(gy, 4)
+        u, v = x + self.core * (z - x), z + self.core * (x - z)
+        self.pos = {"y": lax.div(gx, 2), "z": z, "x": x, "u": u, "v": v}
 
     def peer(self, axis, d):
         q = lax.rem(self.pos[axis] + d, 4)
         if axis == "y":
             return (q * 2 + self.core, self.gy)
+        if axis in ("u", "v"):
+            x, z = self.pos["x"], self.pos["z"]
+            turned = self.core if axis == "u" else 1 - self.core
+            return (self.gx, (z + turned * (q - z)) * 4 + x + (1 - turned) * (q - x))
         if axis == "z":
             return (self.gx, q * 4 + self.pos["x"])
         return (self.gx, self.pos["z"] * 4 + q)
@@ -214,10 +220,10 @@
 
 def step_kernel(
     features_hbm, weight_hbm, second_hbm, centres_hbm, active, labels,
-    loss, grad_first, grad_second, grad_centres,
-    features, weight, second, centres, sends, blocks, turned, nh, nht, expt,
-    hid, act, act_t, slope, uh, inv_embed, gu, ge, first,
-    sums, got, places, spots, where_found, held0, held1, wide0, wide1, pair0, pair1, local_sem, out_sem, a2a_send, a2a_recv, pair_send, pair_recv, *bufs,
+    loss, grad_first, grad_second, nh,
+    features, weight, second, centres, sends, blocks, turned, nht, expt,
+    hid, act, act_t, slope, uh, inv_embed, gu, ge,
+    sums, got, places, spots, where_found, held0, held1, pair0, pair1, local_sem, a2a_send, a2a_recv, pair_send, pair_recv, *bufs,
 ):
     size = len(bufs) // (2 * PARTS)
     sets = [bufs[k * size : (k + 1) * size] for k in range(2 * PARTS)]
@@ -227,18 +233,24 @@
     device = me * 16 + place.gy
     gut = held0
     loads = [
-        pltpu.make_async_copy(src, dst, local_sem.at[i])
+        pltpu.make_async_copy(src, dst, local_sem.at[2 + i])
         for i, (src, dst) in enumerate(
-            ((features_hbm, features), (centres_hbm, centres), (weight_hbm, weight), (second_hbm, second))
+            ((centres_hbm, centres), (weight_hbm, weight), (second_hbm, second))
         )
     ]
 
     def prepare():
-        for load in loads:
-            load.start()
-        loads[0].wait()
-        for j in range(8):
-            sends[j] = features[:, j * BLOCK : (j + 1) * BLOCK]
+        for k in range(2):
+            wide = pltpu.make_async_copy(
+                features_hbm.at[:, pl.ds(k * 4 * BLOCK, 4 * BLOCK)], features, local_sem.at[k]
+            )
+            wide.start()
+            if k == 0:
+                for load in loads:
+                    load.start()
+            wide.wait()
+            for j in range(4):
+                sends[4 * k + j] = features[:, j * BLOCK : (j + 1) * BLOCK]
 
     place.greet(prepare)
     def exchange(part):
@@ -260,7 +272,7 @@
             places[:, spot : spot + SHARE] = labels[:, j * 128 + low : j * 128 + low + SHARE]
     sums[...] = jnp.zeros_like(sums)
     where_found[...] = jnp.full_like(where_found, -1.0)
-    loads[1].wait()
+    loads[0].wait()
 
     def normalise(i):
         rows = block(i, 128)
@@ -300,7 +312,7 @@
         uh[rows, :] = u.astype(BF16)
 
     def locate(i):
-        row = active[:, block(i, 128)] + device * CLS_DEV
+        row = active[block(i, 128)].reshape(1, 128) + device * CLS_DEV
         column = jnp.transpose(jnp.broadcast_to(row, (128, 128)))
         here = (lax.broadcasted_iota(jnp.int32, (128, 128), 0) + i * 128).astype(F32)
         for part in range(0, IMAGES, 128):
@@ -312,7 +324,7 @@
     def columns(i):
         parts = []
         for k in range(TILE // 128):
-            row = active[:, block(i * (TILE // 128) + k, 128)] + device * CLS_DEV
+            row = active[block(i * (TILE // 128) + k, 128)].reshape(1, 128) + device * CLS_DEV
             parts.append(jnp.transpose(jnp.broadcast_to(row, (128, 128))))
         return jnp.concatenate(parts, axis=0)
 
@@ -442,32 +454,33 @@
     done = [0]
 
     def pull(i, held):
-        held[...] = jnp.dot(expt[block(i, TILE), :], uh[...], preferred_element_type=F32)
+        result = jnp.dot(expt[block(i, TILE), :], uh[...], preferred_element_type=F32)
+        held[:TILE, :] = result[:, :PART]
+        held[TILE:, :] = result[:, PART:]
 
     def centre(i, held):
         rows = block(i, TILE)
         cen = centres[rows, :].astype(F32)
         inv = lax.rsqrt(jnp.sum(cen * cen, axis=1, keepdims=True) + NORM_EPSILON)
         normed = cen * inv
-        grad_normed = held[...]
+        grad_normed = jnp.concatenate([held[:TILE, :], held[TILE:, :]], axis=1)
         along = jnp.sum(grad_normed * normed, axis=1, keepdims=True)
         nh[rows, :] = (inv * (grad_normed - normed * along)).astype(BF16)
-        pltpu.make_async_copy(nh.at[rows], grad_centres.at[rows], out_sem.at[0]).start()
 
     def centre_grads(count):
         if done[0] == 0:
-            pull(0, wide0)
+            pull(0, held0)
 
         def step(i):
-            pull(2 * i + 1, wide1)
-            centre(2 * i, wide0)
-            pull(2 * i + 2, wide0)
-            centre(2 * i + 1, wide1)
+            pull(2 * i + 1, held1)
+            centre(2 * i, held0)
+            pull(2 * i + 2, held0)
+            centre(2 * i + 1, held1)
 
         each(count, step, done[0])
         done[0] += count
         if done[0] == 9:
-            centre(18, wide0)
+            centre(18, held0)
 
     def finish(part):
         rows = slice(part * PART, part * PART + PART)
@@ -481,34 +494,17 @@
         )
         act[rows, :] = (grad_act * slope[rows, :]).astype(BF16)
 
-    def early(_):
-        known = slice(0, IMAGES - PART)
-
+    def weights():
         def rows_of_first(i):
             rows = block(i, 288)
-            first[rows, :] = jnp.dot(turned[rows, known], act[known, :], preferred_element_type=F32)
-
-        each(3, rows_of_first)
-
-    def late(_):
-        new = slice(IMAGES - PART, IMAGES)
-
-        def rows_of_first(i):
-            rows = block(i, 288)
-            more = jnp.dot(turned[rows, new], act[new, :], preferred_element_type=F32)
-            turned[rows, 0:HIDDEN] = (first[rows, :] + more).astype(BF16)
+            grad_first[rows, :] = jnp.dot(turned[rows, :], act[...], preferred_element_type=F32).astype(BF16)
 
         def rows_of_second(i):
             rows = block(i, 256)
-            act_t[rows, 0:EMBED] = jnp.dot(act_t[rows, :], ge[...], preferred_element_type=F32).astype(BF16)
+            grad_second[rows, :] = jnp.dot(act_t[rows, :], ge[...], preferred_element_type=F32).astype(BF16)
 
         each(3, rows_of_first)
-        leaving = [pltpu.make_async_copy(turned.at[:, pl.ds(0, HIDDEN)], grad_first, local_sem.at[4])]
-        leaving[0].start()
         each(3, rows_of_second)
-        leaving.append(pltpu.make_async_copy(act_t.at[:, pl.ds(0, EMBED)], grad_second, local_sem.at[5]))
-        leaving[1].start()
-        return leaving
 
     def go(steps):
         next(steps, None)
@@ -530,7 +526,7 @@
     each(24, normalise)
     exchange(1)
     each(CENTRES // 128 - 24, normalise, 24)
-    loads[2].wait()
+    loads[1].wait()
     begin(0)
     each(2, turn)
     go(c[0])
@@ -556,7 +552,7 @@
     each(2, turn, 6)
     go(c[1])
     go(c[3])
-    loads[3].wait()
+    loads[2].wait()
     go(c[0])
     go(c[2])
     go(c[0])
@@ -636,57 +632,44 @@
     go(r[2])
     centre_grads(2)
     go(r[0])
+    go(r[3])
     go(r[1])
+    go(r[2])
     go(r[0])
-    go(r[2])
+    centre_grads(1)
     finish(0)
+    centre_grads(1)
     go(r[3])
-    centre_grads(1)
     go(r[1])
     go(r[2])
     centre_grads(1)
     go(r[1])
-    go(r[3])
     finish(1)
     centre_grads(1)
-    go(r[2])
     go(r[3])
     go(r[2])
+    centre_grads(1)
+    go(r[2])
     finish(2)
-    centre_grads(1)
-    early(0)
     go(r[3])
     centre_grads(2)
     go(r[3])
-    centre_grads(1)
     go(r[3])
     finish(3)
-    leaving = late(0)
+    weights()
 
     for part in range(PARTS):
         landed(blocks.at[pl.ds(0, 7 * SHARE)], a2a_send.at[part])
-    for copy in leaving:
-        copy.wait()
-    landed(nh, out_sem.at[0])
-
-
-def last_kernel(
-    first_hbm, second_hbm, centres_hbm, loss_in,
-    loss, grad_first, grad_second, grad_centres,
-    first, second, held, in_sem, out_sem,
-):
-    parts = [pl.ds(k * (CENTRES // 8), CENTRES // 8) for k in range(8)]
-    ways = [(centres_hbm.at[p], held.at[p], grad_centres.at[p]) for p in parts]
-    ways += [(first_hbm, first, grad_first), (second_hbm, second, grad_second)]
-    arrive = [pltpu.make_async_copy(w[0], w[1], in_sem.at[k]) for k, w in enumerate(ways)]
-    depart = [pltpu.make_async_copy(w[1], w[2], out_sem.at[k]) for k, w in enumerate(ways)]
-    for copy in arrive:
+
+
+def last_kernel(first, second, held, loss_in, loss, grad_first, grad_second, grad_centres, sem):
+    parts = [pl.ds(k * (CENTRES // 4), CENTRES // 4) for k in range(4)]
+    ways = [(held.at[p], grad_centres.at[p]) for p in parts] + [(first, grad_first), (second, grad_second)]
+    copies = [pltpu.make_async_copy(src, dst, sem.at[k]) for k, (src, dst) in enumerate(ways)]
+    for copy in copies:
         copy.start()
     loss[...] = loss_in[...]
-    for there, back in zip(arrive, depart):
-        there.wait()
-        back.start()
-    for copy in depart:
+    for copy in copies:
         copy.wait()
 
 
@@ -698,21 +681,20 @@
         step_kernel,
         out_shape=(
             jax.ShapeDtypeStruct((1, 1), F32),
-            jax.ShapeDtypeStruct((BLOCK, HIDDEN), BF16),
-            jax.ShapeDtypeStruct((HIDDEN, EMBED), BF16),
-            jax.ShapeDtypeStruct((CENTRES, EMBED), BF16),
+            pltpu.VMEM((BLOCK, HIDDEN), BF16),
+            pltpu.VMEM((HIDDEN, EMBED), BF16),
+            pltpu.VMEM((CENTRES, EMBED), BF16),
         ),
         in_specs=[in_place] * 4 + [near] * 2,
-        out_specs=(near,) + (in_place,) * 3,
+        out_specs=(near,) * 4,
         scratch_shapes=[
-            pltpu.VMEM((128, 8 * BLOCK), BF16),
+            pltpu.VMEM((128, 4 * BLOCK), BF16),
             pltpu.VMEM((BLOCK, HIDDEN), BF16),
             pltpu.VMEM((HIDDEN, EMBED), BF16),
             pltpu.VMEM((CENTRES, EMBED), BF16),
             pltpu.VMEM((8, 128, BLOCK), BF16),
             pltpu.VMEM((IMAGES, BLOCK), BF16),
             pltpu.VMEM((BLOCK, IMAGES), BF16),
-            pltpu.VMEM((CENTRES, EMBED), BF16),
             pltpu.VMEM((EMBED, CENTRES), BF16),
             pltpu.VMEM((CENTRES, IMAGES), BF16),
             pltpu.VMEM((6, IMAGES, 128), BF16),
@@ -723,7 +705,6 @@
             pltpu.VMEM((IMAGES, 1), F32),
             pltpu.VMEM((4, IMAGES, 128), BF16),
             pltpu.VMEM((IMAGES, EMBED), BF16),
-            pltpu.VMEM((BLOCK, HIDDEN), F32),
             pltpu.VMEM((2, 8, IMAGES), F32),
             pltpu.VMEM((PARTS, 4, 4, 2, PART), F32),
             pltpu.VMEM((1, IMAGES), jnp.int32),
@@ -731,12 +712,9 @@
             pltpu.VMEM((8, IMAGES), F32),
             pltpu.VMEM((2 * TILE, PART), F32),
             pltpu.VMEM((2 * TILE, PART), F32),
-            pltpu.VMEM((TILE, EMBED), F32),
-            pltpu.VMEM((TILE, EMBED), F32),
             pltpu.VMEM((2 * TILE, PART), BF16),
             pltpu.VMEM((2 * TILE, PART), BF16),
-            dma((6,)),
-            dma((1,)),
+            dma((5,)),
             dma((PARTS,)),
             dma((PARTS,)),
             dma((PARTS, 4)),
@@ -745,14 +723,14 @@
         + sum_scratch(3) * PARTS
         + sum_scratch(2) * PARTS,
         compiler_params=pltpu.CompilerParams(
-            collective_id=0, has_side_effects=True, vmem_limit_bytes=67043328
+            collective_id=0, has_side_effects=True, vmem_limit_bytes=59600000
         ),
     )(
         features,
         first_weight,
         second_weight,
         centres,
-        active.reshape(1, CENTRES),
+        active,
         labels.reshape(1, IMAGES),
     )
     loss, grad_first, grad_second, grad_centres = pl.pallas_call(
@@ -763,16 +741,10 @@
             jax.ShapeDtypeStruct((HIDDEN, EMBED), BF16),
             jax.ShapeDtypeStruct((CENTRES, EMBED), BF16),
         ),
-        in_specs=[in_place] * 3 + [near],
+        in_specs=[near] * 4,
         out_specs=(near,) + (in_place,) * 3,
-        scratch_shapes=[
-            pltpu.VMEM((BLOCK, HIDDEN), BF16),
-            pltpu.VMEM((HIDDEN, EMBED), BF16),
-            pltpu.VMEM((CENTRES, EMBED), BF16),
-            dma((10,)),
-            dma((10,)),
-        ],
-        compiler_params=pltpu.CompilerParams(vmem_limit_bytes=60000000),
+        scratch_shapes=[dma((6,))],
+        compiler_params=pltpu.CompilerParams(vmem_limit_bytes=16000000),
     )(first, second, grads, loss)
     return loss.reshape(()), grad_first, grad_second, grad_centres
 

time: 119 us -> 114 us (0.958)
  Pallas kernels: 116 us -> 113 us
  local copies, waits for them, and re-layouts: 1.35 us -> 0 us
    pallas_call x1, Pallas kernels: 7.16 us -> 4.11 us  [shards(): pl.pallas_call(last_kernel, out_shape=(jax.ShapeDtypeStruct((1, 1), F32),...]
    reshape x1 -> x0, local copies, waits for them, and re-layouts: 1.35 us -> none  [shards(): active.reshape(1, CENTRES)]
where the time goes in v6:
time: 114 us
  Pallas kernels  113 us (99%)
    pallas_call x1, Pallas kernels, shards(): pl.pallas_call(step_kernel, out_shape=(jax.ShapeDtypeStruct((1, 1), F32),...  109 us
    pallas_call x1, Pallas kernels, shards(): pl.pallas_call(last_kernel, out_shape=(jax.ShapeDtypeStruct((1, 1), F32),...  4.11 us

profile of v6, /device:TPU:1, one launch (start us, length us, event | category | flops | bytes accessed | tf_op | source)
XLA Modules:
  0.0 113.8 jit_solution(7079868306227588738)
XLA Ops:
  0.6 108.9 %shard_map.93 = (f32[1,1]{1,0:T(1,128)}, bf16[864,768]{1,0:T(8,128)(2,1)S(1)}, bf16[768,512]{1,0:T(8,128)(2,1)S(1)}, bf16[4864,512]{1,0:T(8,128)(2,1)S(1)}) custom-call(bf16[128,6912]{1,0:T(8,128)(2,1)} %features_hbm.1, bf16[864,768]{1,0:T(8,128)(2,1)} %weight_hbm.1, bf16[768,512]{1,0:T(8,128)(2,1)} %second_hbm.1, bf16[4864,512]{1,0:T(8,128)(2,1)} %centres_hbm.1, ...), custom_call_target="tpu_custom_call" | custom-call | tf_op jit(solution)/shard_map/pallas_call | solution.py:680
  109.6 4.1 %shard_map.94 = (f32[1,1]{1,0:T(1,128)}, bf16[864,768]{1,0:T(8,128)(2,1)}, bf16[768,512]{1,0:T(8,128)(2,1)}, bf16[4864,512]{1,0:T(8,128)(2,1)}) custom-call(bf16[864,768]{1,0:T(8,128)(2,1)S(1)} %get-tuple-element.12.first, bf16[768,512]{1,0:T(8,128)(2,1)S(1)} %get-tuple-element.13.second, bf16[4864,512]{1,0:T(8,128)(2,1)S(1)} %get-tuple-element.14.held, ...), custom_call_target="tpu_custom_call" | custom-call | tf_op jit(solution)/shard_map/pallas_call | solution.py:736

commit v7 on v6

--- a/solution.py
+++ b/solution.py
@@ -494,17 +494,36 @@
         )
         act[rows, :] = (grad_act * slope[rows, :]).astype(BF16)
 
-    def weights():
+    def early():
+        known = slice(0, IMAGES - PART)
+
         def rows_of_first(i):
             rows = block(i, 288)
-            grad_first[rows, :] = jnp.dot(turned[rows, :], act[...], preferred_element_type=F32).astype(BF16)
-
-        def rows_of_second(i):
-            rows = block(i, 256)
-            grad_second[rows, :] = jnp.dot(act_t[rows, :], ge[...], preferred_element_type=F32).astype(BF16)
+            grad_first[rows, :] = jnp.dot(
+                turned[rows, known], act[known, :], preferred_element_type=F32
+            ).astype(BF16)
 
         each(3, rows_of_first)
-        each(3, rows_of_second)
+        for i in range(3):
+            rows = slice(i * 256, i * 256 + 256)
+            result = jnp.dot(act_t[rows, known], ge[known, :], preferred_element_type=F32)
+            for n in range(4):
+                one[n][0][i] = result[:, n * 128 : (n + 1) * 128]
+
+    def late():
+        new = slice(IMAGES - PART, IMAGES)
+
+        def rows_of_first(i):
+            rows = block(i, 288)
+            more = jnp.dot(turned[rows, new], act[new, :], preferred_element_type=F32)
+            grad_first[rows, :] = (grad_first[rows, :].astype(F32) + more).astype(BF16)
+
+        each(3, rows_of_first)
+        for i in range(3):
+            rows = slice(i * 256, i * 256 + 256)
+            more = jnp.dot(act_t[rows, new], ge[new, :], preferred_element_type=F32)
+            known = jnp.concatenate([one[n][0][i] for n in range(4)], axis=1)
+            grad_second[rows, :] = (known + more).astype(BF16)
 
     def go(steps):
         next(steps, None)
@@ -652,11 +671,13 @@
     go(r[2])
     finish(2)
     go(r[3])
-    centre_grads(2)
+    centre_grads(1)
+    early()
     go(r[3])
+    centre_grads(1)
     go(r[3])
     finish(3)
-    weights()
+    late()
 
     for part in range(PARTS):
         landed(blocks.at[pl.ds(0, 7 * SHARE)], a2a_send.at[part])

time: 114 us -> 112 us (0.982)
  Pallas kernels: 113 us -> 111 us
    pallas_call x1, Pallas kernels: 109 us -> 107 us  [shards(): pl.pallas_call(step_kernel, out_shape=(jax.ShapeDtypeStruct((1, 1), F32),...]
where the time goes in v7:
time: 112 us
  Pallas kernels  111 us (99%)
    pallas_call x1, Pallas kernels, shards(): pl.pallas_call(step_kernel, out_shape=(jax.ShapeDtypeStruct((1, 1), F32),...  107 us
    pallas_call x1, Pallas kernels, shards(): pl.pallas_call(last_kernel, out_shape=(jax.ShapeDtypeStruct((1, 1), F32),...  4.11 us

profile of v7, /device:TPU:1, one launch (start us, length us, event | category | flops | bytes accessed | tf_op | source)
XLA Modules:
  0.0 111.9 jit_solution(14279840555903447455)
XLA Ops:
  0.6 107.0 %shard_map.93 = (f32[1,1]{1,0:T(1,128)}, bf16[864,768]{1,0:T(8,128)(2,1)S(1)}, bf16[768,512]{1,0:T(8,128)(2,1)S(1)}, bf16[4864,512]{1,0:T(8,128)(2,1)S(1)}) custom-call(bf16[128,6912]{1,0:T(8,128)(2,1)} %features_hbm.1, bf16[864,768]{1,0:T(8,128)(2,1)} %weight_hbm.1, bf16[768,512]{1,0:T(8,128)(2,1)} %second_hbm.1, bf16[4864,512]{1,0:T(8,128)(2,1)} %centres_hbm.1, ...), custom_call_target="tpu_custom_call" | custom-call | tf_op jit(solution)/shard_map/pallas_call | solution.py:701
  107.6 4.1 %shard_map.94 = (f32[1,1]{1,0:T(1,128)}, bf16[864,768]{1,0:T(8,128)(2,1)}, bf16[768,512]{1,0:T(8,128)(2,1)}, bf16[4864,512]{1,0:T(8,128)(2,1)}) custom-call(bf16[864,768]{1,0:T(8,128)(2,1)S(1)} %get-tuple-element.12.first, bf16[768,512]{1,0:T(8,128)(2,1)S(1)} %get-tuple-element.13.second, bf16[4864,512]{1,0:T(8,128)(2,1)S(1)} %get-tuple-element.14.held, ...), custom_call_target="tpu_custom_call" | custom-call | tf_op jit(solution)/shard_map/pallas_call | solution.py:757
